TPU v7x, 32 devices: a whole 2x2x4 slice. The times are simulated.
32 devices in a mesh: row: 16 (over z, x, core), col: 2 (over y).
Axes of the slice: x: 2, y: 2, z: 4, core: 2. Of those that a mesh axis runs over, the one named last changes fastest.
Arguments:
- counts: int32 [8192, 32768], P('row', 'col'), may hold values from 0 to 63
- row_support: int32 [8192], P(('row', 'col')), may hold values from 1 to 2209
- col_support: int32 [32768], P(('col', 'row')), may hold values from 1 to 2209
- total: int32 [1], replicated, may hold values from 256 to 4095
- sketch: bfloat16 [32768, 256], P('col'), may hold values from -6 to 6
Outputs:
- left_basis: float32 [8192, 256], P('row')
- right_basis: float32 [32768, 256], P('col')
All inputs are finite; a program needn't handle non-finite values.
Results may differ from a plain program's by a relative error of at most 0.012.
Values may be sent and summed in bfloat16 or wider, within the bound.
A program may use at most 192 MiB of HBM per device.

v0:
```python
import jax
import jax.numpy as jnp
from jax import lax
from jax.sharding import PartitionSpec as P


def lift(block, row_part, col_part, total):
    value = jnp.log(jnp.maximum(block, 1).astype(jnp.float32))
    value = value + jnp.log(total[0].astype(jnp.float32))
    value = value - jnp.log(row_part.astype(jnp.float32))[:, None]
    value = value - jnp.log(col_part.astype(jnp.float32))[None, :]
    return jnp.where(block > 0, jnp.maximum(value, 0.0), 0.0).astype(jnp.bfloat16)


def factor_of(gram):
    return jnp.linalg.cholesky(gram)


def solve_rows(lower, matrix):
    return jax.scipy.linalg.solve_triangular(lower, matrix.T, lower=True).T


def gram_of(matrix):
    return jnp.dot(matrix.T, matrix, precision=lax.Precision.HIGHEST)


def per_device(counts, row_support, col_support, total, sketch):
    row_local = lax.all_gather(row_support, "col", axis=0, tiled=True)
    col_local = lax.all_gather(col_support, "row", axis=0, tiled=True)
    table = lift(counts, row_local, col_local, total)
    row_count = table.shape[0]
    col_count = table.shape[1]

    def left_orth(rhs, narrow):
        whole = lax.psum(jnp.dot(table, rhs, preferred_element_type=jnp.float32), "col")
        gram = lax.psum(gram_of(whole), "row")
        basis = solve_rows(factor_of(gram), whole)
        if narrow:
            return basis.astype(jnp.bfloat16)
        return basis

    q_first = left_orth(sketch, True)
    partial_value = lax.dot_general(
        table, q_first, (((0,), (0,)), ((), ())), preferred_element_type=jnp.float32
    )
    whole = lax.psum(partial_value, "row")
    gram = lax.psum(gram_of(whole), "col")
    q_second = solve_rows(factor_of(gram), whole)
    q_third = left_orth(q_second.astype(jnp.bfloat16), False)
    total_rows = row_count * lax.axis_size("row")
    total_cols = col_count * lax.axis_size("col")
    return (
        q_third * jnp.sqrt(jnp.float32(total_rows)),
        q_second * jnp.sqrt(jnp.float32(total_cols)),
    )


def solution(mesh):
    in_specs = (P("row", "col"), P(("row", "col")), P(("col", "row")), P(), P("col", None))
    out_specs = (P("row", None), P("col", None))
    return jax.shard_map(
        per_device, mesh=mesh, in_specs=in_specs, out_specs=out_specs, check_vma=False
    )
```

profile of v0, /device:TPU:0, one launch (start us, length us, event | category | flops | bytes accessed | tf_op | source)
XLA Modules:
  0.0 932.7 jit_solution(9221446948077840741)
XLA Ops:
  7.2 23.5 %all_gather.7 = s32[16384]{0:T(1024)S(1)} all-gather(s32[1024]{0:T(1024)} %param.10), channel_id=1, replica_groups=mesh['row'=16,'col'=2] {'row'}, dimensions={0}, use_global_device_ids=true | all-gather | bytes 69632 | tf_op jit(solution)/shard_map/all_gather | solution.py:29
  30.7 4.5 all-gather
  35.9 17.1 %select_convert_fusion = bf16[512,16384]{1,0:T(8,128)(2,1)S(1)} fusion(s32[512,16384]{1,0:T(8,128)} %param.8, f32[16384]{0:T(1024)S(1)} %convert_log_fusion, f32[512]{0:T(512)S(1)} %bitcast.119, f32[]{:T(128)} %bitcast), kind=kLoop, calls=%fused_computation.6 | loop fusion | flops 75497472 | bytes 50399236 | tf_op jit(solution)/shard_map/convert_element_type | solution.py:12
  53.0 6.2 copy-done.2
  59.2 7.7 fusion.42
  67.0 26.0 %all-reduce.8.cloned.1.call-done = f32[512,256]{1,0:T(8,128)} async-done(((f32[512,256]{1,0:T(8,128)}), f32[512,256]{1,0:T(8,128)}) %all-reduce.8.cloned.1.call-update) | async-done | bytes 524304 | tf_op jit(solution)/shard_map/psum | solution.py:35
  93.0 2.9 fusion.43
  96.2 90.5 %all-reduce.10.cloned.1.call-done = f32[256,256]{0,1:T(8,128)} async-done(((f32[256,256]{0,1:T(8,128)}), f32[256,256]{0,1:T(8,128)}) %all-reduce.10.cloned.1.call-update) | async-done | bytes 262160 | tf_op jit(solution)/shard_map/psum | solution.py:36
  186.8 1.1 copy.16
  188.8 11.7 %cholesky.172 = f32[128,128]{1,0:T(8,128)S(1)} custom-call(f32[128,128]{1,0:T(8,128)S(1)} %cholesky.270), custom_call_target="Cholesky" | custom-call | tf_op jit(solution)/shard_map/jit(cholesky)/cholesky | solution.py:16
  200.6 9.8 %custom-call.19 = f32[1,128,128]{1,2,0:T(8,128)S(1)} custom-call(f32[1,128,128]{2,1,0:T(8,128)S(1)} %get-tuple-element.73), custom_call_target="InvertDiagBlocksLowerTriangular" | custom-call | tf_op jit(solution)/shard_map/jit(cholesky)/cholesky | solution.py:16
  210.9 11.7 %cholesky.189 = f32[128,128]{1,0:T(8,128)S(1)} custom-call(f32[128,128]{1,0:T(8,128)S(1)} %convolution_subtract_fusion.5), custom_call_target="Cholesky" | custom-call | tf_op jit(solution)/shard_map/jit(cholesky)/cholesky | solution.py:16
  224.9 4.5 while.6
  225.9 1.4 bitcast_dynamic-update-slice_fusion.7
  227.9 1.4 bitcast_dynamic-update-slice_fusion.7
  229.4 19.7 %custom-call.20 = f32[2,128,128]{1,2,0:T(8,128)S(1)} custom-call(f32[2,128,128]{2,1,0:T(8,128)S(1)} %get-tuple-element.26), custom_call_target="InvertDiagBlocksLowerTriangular" | custom-call | tf_op jit(solution)/shard_map/jit(_solve_triangular)/triangular_solve | solution.py:20
  249.1 1.4 fusion.9
  250.4 1.5 convolution_subtract_fusion.2
  252.4 16.1 %fusion.6 = f32[16384,256]{1,0:T(8,128)} fusion(bf16[512,16384]{1,0:T(8,128)(2,1)} %copy-done.2, bf16[128,512]{1,0:T(8,128)(2,1)S(1)} %fusion.23, f32[128,512]{1,0:T(8,128)S(1)} %fusion.9), kind=kOutput, calls=%fused_computation.25 | convolution fusion | flops 4295491584 | bytes 33947648 | tf_op jit(solution)/shard_map/dot_general | solution.py:43
  268.6 298.5 %all-reduce.12.cloned.1.call-done = f32[16384,256]{1,0:T(8,128)} async-done(((f32[16384,256]{1,0:T(8,128)}), f32[16384,256]{1,0:T(8,128)}) %all-reduce.12.cloned.1.call-update) | async-done | bytes 16777232 | tf_op jit(solution)/shard_map/psum | solution.py:46
  567.1 37.8 %fusion.44 = f32[256,256]{0,1:T(8,128)} fusion(f32[16384,256]{1,0:T(8,128)} %all-reduce.12.cloned.1.call-done), kind=kOutput, calls=%fused_computation.95 | convolution fusion | flops 12884901888 | bytes 17039360 | tf_op jit(solution)/shard_map/dot_general | solution.py:24
  605.0 23.0 %all-reduce.14.cloned.1.call-done = f32[256,256]{0,1:T(8,128)} async-done(((f32[256,256]{0,1:T(8,128)}), f32[256,256]{0,1:T(8,128)}) %all-reduce.14.cloned.1.call-update) | async-done | bytes 262160 | tf_op jit(solution)/shard_map/psum | solution.py:47
  628.0 1.1 copy.18
  630.1 11.7 %cholesky.206 = f32[128,128]{1,0:T(8,128)S(1)} custom-call(f32[128,128]{1,0:T(8,128)S(1)} %cholesky.273), custom_call_target="Cholesky" | custom-call | tf_op jit(solution)/shard_map/jit(cholesky)/cholesky | solution.py:16
  641.9 9.8 %custom-call.21 = f32[1,128,128]{1,2,0:T(8,128)S(1)} custom-call(f32[1,128,128]{2,1,0:T(8,128)S(1)} %get-tuple-element.69), custom_call_target="InvertDiagBlocksLowerTriangular" | custom-call | tf_op jit(solution)/shard_map/jit(cholesky)/cholesky | solution.py:16
  652.2 11.7 %cholesky.223 = f32[128,128]{1,0:T(8,128)S(1)} custom-call(f32[128,128]{1,0:T(8,128)S(1)} %convolution_subtract_fusion.4), custom_call_target="Cholesky" | custom-call | tf_op jit(solution)/shard_map/jit(cholesky)/cholesky | solution.py:16
  666.5 3.8 while.5
  667.1 1.3 bitcast_dynamic-update-slice_fusion.6
  669.0 1.3 bitcast_dynamic-update-slice_fusion.6
  670.3 19.7 %custom-call.15 = f32[2,128,128]{1,2,0:T(8,128)S(1)} custom-call(f32[2,128,128]{2,1,0:T(8,128)S(1)} %get-tuple-element.19), custom_call_target="InvertDiagBlocksLowerTriangular" | custom-call | tf_op jit(solution)/shard_map/jit(_solve_triangular)/triangular_solve | solution.py:20
  690.0 10.8 %fusion.3 = f32[128,16384]{1,0:T(8,128)S(1)} fusion(f32[256,16384]{0,1:T(8,128)} %bitcast.113, f32[2,128,128]{1,2,0:T(8,128)S(1)} %custom-call.15), kind=kOutput, calls=%fused_computation.12 | convolution fusion | flops 3221225472 | bytes 16842752 | tf_op jit(solution)/shard_map/jit(_solve_triangular)/triangular_solve | solution.py:20
  700.8 13.4 %convolution_subtract_fusion = f32[128,16384]{0,1:T(8,128)S(1)} fusion(f32[128,16384]{1,0:T(8,128)S(1)} %fusion.3, f32[256,16384]{0,1:T(8,128)S(1)} %bitcast.114, f32[256,256]{1,0:T(8,128)S(1)} %get-tuple-element.225), kind=kOutput, calls=%fused_computation.7 | convolution fusion | flops 3223322624 | bytes 25231360 | tf_op jit(solution)/shard_map/jit(_solve_triangular)/triangular_solve | solution.py:20
  714.2 9.8 %fusion.19 = f32[128,16384]{1,0:T(8,128)} fusion(f32[128,16384]{0,1:T(8,128)S(1)} %convolution_subtract_fusion, f32[2,128,128]{1,2,0:T(8,128)S(1)} %custom-call.15), kind=kOutput, calls=%fused_computation.45 | convolution fusion | flops 3221225472 | bytes 16842752 | tf_op jit(solution)/shard_map/jit(_solve_triangular)/triangular_solve | solution.py:20
  724.0 13.7 %fusion.1 = f32[512,256]{1,0:T(8,128)} fusion(bf16[512,16384]{1,0:T(8,128)(2,1)} %copy-done.2, f32[128,16384]{1,0:T(8,128)} %fusion.19, f32[128,16384]{1,0:T(8,128)} %copy-done.1), kind=kOutput, calls=%fused_computation.11 | convolution fusion | flops 4311744512 | bytes 34078720 | tf_op jit(solution)/shard_map/dot_general | solution.py:35
  737.8 28.8 %all-reduce.16.cloned.1.call-done = f32[512,256]{1,0:T(8,128)} async-done(((f32[512,256]{1,0:T(8,128)}), f32[512,256]{1,0:T(8,128)}) %all-reduce.16.cloned.1.call-update) | async-done | bytes 524304 | tf_op jit(solution)/shard_map/psum | solution.py:35
  766.6 2.9 fusion.45
  769.5 12.1 %multiply_bitcast_fusion = f32[16384,256]{0,1:T(8,128)} fusion(f32[128,16384]{1,0:T(8,128)} %fusion.19, f32[128,16384]{1,0:T(8,128)} %copy-done.1), kind=kLoop, calls=%fused_computation.9 | loop fusion | flops 8388608 | bytes 33554432 | tf_op jit(solution)/shard_map/mul | solution.py:54
  781.6 17.5 %copy.22 = f32[16384,256]{1,0:T(8,128)} copy(f32[16384,256]{0,1:T(8,128)} %multiply_bitcast_fusion) | data formatting | bytes 33554432
  799.2 61.0 %all-reduce.18.cloned.1.call-done = f32[256,256]{0,1:T(8,128)} async-done(((f32[256,256]{0,1:T(8,128)}), f32[256,256]{0,1:T(8,128)}) %all-reduce.18.cloned.1.call-update) | async-done | bytes 262160 | tf_op jit(solution)/shard_map/psum | solution.py:36
  860.1 1.1 copy.20
  862.2 11.7 %cholesky.240 = f32[128,128]{1,0:T(8,128)S(1)} custom-call(f32[128,128]{1,0:T(8,128)S(1)} %cholesky.276), custom_call_target="Cholesky" | custom-call | tf_op jit(solution)/shard_map/jit(cholesky)/cholesky | solution.py:16
  874.0 9.8 %custom-call.22 = f32[1,128,128]{1,2,0:T(8,128)S(1)} custom-call(f32[1,128,128]{2,1,0:T(8,128)S(1)} %get-tuple-element.65), custom_call_target="InvertDiagBlocksLowerTriangular" | custom-call | tf_op jit(solution)/shard_map/jit(cholesky)/cholesky | solution.py:16
  884.3 11.7 %cholesky.257 = f32[128,128]{1,0:T(8,128)S(1)} custom-call(f32[128,128]{1,0:T(8,128)S(1)} %convolution_subtract_fusion.3), custom_call_target="Cholesky" | custom-call | tf_op jit(solution)/shard_map/jit(cholesky)/cholesky | solution.py:16
  898.8 4.1 while.7
  899.4 1.4 bitcast_dynamic-update-slice_fusion.8
  901.5 1.4 bitcast_dynamic-update-slice_fusion.8
  902.9 20.0 %custom-call.23 = f32[2,128,128]{1,2,0:T(8,128)S(1)} custom-call(f32[2,128,128]{2,1,0:T(8,128)S(1)} %get-tuple-element.27), custom_call_target="InvertDiagBlocksLowerTriangular" | custom-call | tf_op jit(solution)/shard_map/jit(_solve_triangular)/triangular_solve | solution.py:20
  924.4 1.0 copy.21
  (72 shorter events, 14.3 us)
Async XLA Ops:
  7.2 85.9 %all-reduce.8.cloned.1.call-start = ((), (), s32[]{:S(2)}) async-start(), calls=%async_computation | async-start | bytes 1048576 | tf_op jit(solution)/shard_map/psum | solution.py:35
  53.0 6.2 copy-start.2
  67.0 119.8 %all-reduce.10.cloned.1.call-start = ((), (), s32[]{:S(2)}) async-start(), calls=%async_computation.1 | async-start | bytes 524288 | tf_op jit(solution)/shard_map/psum | solution.py:36
  96.0 471.1 %all-reduce.12.cloned.1.call-start = ((), (), s32[]{:S(2)}) async-start(), calls=%async_computation.2 | async-start | bytes 33554432 | tf_op jit(solution)/shard_map/psum | solution.py:46
  268.5 359.5 %all-reduce.14.cloned.1.call-start = ((), (), s32[]{:S(2)}) async-start(), calls=%async_computation.3 | async-start | bytes 524288 | tf_op jit(solution)/shard_map/psum | solution.py:47
  605.0 161.6 %all-reduce.16.cloned.1.call-start = ((), (), s32[]{:S(2)}) async-start(), calls=%async_computation.4 | async-start | bytes 1048576 | tf_op jit(solution)/shard_map/psum | solution.py:35
  690.0 10.8 %copy-start = (f32[16384,256]{1,0:T(8,128)S(1)}, f32[16384,256]{1,0:T(8,128)}, u32[]{:S(2)}) copy-start(f32[16384,256]{1,0:T(8,128)} %all-reduce.12.cloned.1.call-done) | copy-start | bytes 50331652
  700.8 13.4 %copy-start.1 = (f32[128,16384]{1,0:T(8,128)}, f32[128,16384]{1,0:T(8,128)S(1)}, u32[]{:S(2)}) copy-start(f32[128,16384]{1,0:T(8,128)S(1)} %fusion.3) | copy-start | bytes 25165828
  737.7 122.4 %all-reduce.18.cloned.1.call-start = ((), (), s32[]{:S(2)}) async-start(), calls=%async_computation.5 | async-start | bytes 524288 | tf_op jit(solution)/shard_map/psum | solution.py:36
  781.6 141.2 %copy-start.3 = (f32[512,256]{1,0:T(8,128)S(1)}, f32[512,256]{1,0:T(8,128)}, u32[]{:S(2)}) copy-start(f32[512,256]{1,0:T(8,128)} %all-reduce.16.cloned.1.call-done) | copy-start | bytes 1572868
Sparse Core Ops, SparseCore 0:
  67.1 25.9 all-reduce.7
  97.0 89.7 all-reduce.9
  268.7 298.4 all-reduce.11
  605.1 22.9 all-reduce.13
  737.9 28.6 all-reduce.15
  770.4 89.6 all-reduce.17
where the time goes:
time: 938 us; the launch traced here: 933 us
  waiting for transfers between devices  528 us (56%)
  other arithmetic  195 us (21%)
  matrix products  121 us (13%)
  local copies, waits for them, and re-layouts  40 us (4%)
  blocking collectives  28 us (3%)
  between operations  19.6 us (2%)
    psum x1, waiting for transfers between devices, per_device(): whole = lax.psum(partial_value, 'row')  299 us
    psum x2, waiting for transfers between devices, left_orth(): gram = lax.psum(gram_of(whole), 'row')  151 us
    another operation x20, other arithmetic, factor_of(): return jnp.linalg.cholesky(gram)  103 us
    another operation x7, other arithmetic, solve_rows(): return jax.scipy.linalg.solve_triangular(lower, matrix.T, lower=True).T  59.4 us
    psum x2, waiting for transfers between devices, left_orth(): lax.psum(jnp.dot(table, rhs, preferred_element_type=jnp.float32), 'col')  54.8 us
    dot_general x3, matrix products, gram_of(): return jnp.dot(matrix.T, matrix, precision=lax.Precision.HIGHEST)  43.6 us
    another operation x9, matrix products, solve_rows(): return jax.scipy.linalg.solve_triangular(lower, matrix.T, lower=True).T  38.7 us
    unnamed x10, local copies, waits for them, and re-layouts  24.7 us
  transfers between devices with their start and end apart: 6, of which 6 were waited for; matrix products, arithmetic and copies ran while one was open for 3% of the time, Pallas kernels for 0%

commit v1 on v0

v1 whole, which is shorter than its diff:
```python
import jax
import jax.numpy as jnp
from jax import lax
from jax.experimental import pallas as pl
from jax.experimental.pallas import tpu as pltpu
from jax.sharding import PartitionSpec as P

HIGHEST = lax.Precision.HIGHEST
BLOCK = 32


def lift(block, row_part, col_part, total):
    value = jnp.log(jnp.maximum(block, 1).astype(jnp.float32))
    value = value + jnp.log(total[0].astype(jnp.float32))
    value = value - jnp.log(row_part.astype(jnp.float32))[:, None]
    value = value - jnp.log(col_part.astype(jnp.float32))[None, :]
    return jnp.where(block > 0, jnp.maximum(value, 0.0), 0.0).astype(jnp.bfloat16)


def factor_step(rest, inverse, lower_ref, base):
    size = rest.shape[0]
    lanes = 128
    corner = rest[:BLOCK, :lanes]
    row = lax.broadcasted_iota(jnp.int32, (BLOCK, lanes), 0)
    lane = lax.broadcasted_iota(jnp.int32, (BLOCK, lanes), 1)
    unit = jnp.where(lane - BLOCK == row, 1.0, 0.0)
    work = jnp.where(lane < BLOCK, corner, unit)
    pivots = jnp.ones((BLOCK, 1), jnp.float32)
    for j in range(BLOCK):
        pivot = work[j : j + 1, j : j + 1]
        scaled = work[j : j + 1, :] * (1.0 / pivot)
        column = jnp.where(row > j, work[:, j : j + 1], 0.0)
        work = work - column * scaled
        pivots = jnp.where(row[:, :1] == j, pivot, pivots)
    work = work * lax.rsqrt(pivots)
    small = pltpu.roll(work, lanes - BLOCK, 1)[:, :BLOCK]
    panel = jnp.dot(small, rest[:BLOCK, :], precision=HIGHEST, preferred_element_type=jnp.float32)
    done = jnp.dot(small, inverse[:BLOCK, :], precision=HIGHEST, preferred_element_type=jnp.float32)
    lower_ref[pl.ds(pl.multiple_of(base, BLOCK), BLOCK), :] = done
    panel = pltpu.roll(panel, size - BLOCK, 1)
    down = (((0,), (0,)), ((), ()))
    rest_cut = lax.dot_general(panel, panel, down, precision=HIGHEST, preferred_element_type=jnp.float32)
    inverse_cut = lax.dot_general(panel, done, down, precision=HIGHEST, preferred_element_type=jnp.float32)
    return rest_cut, inverse_cut


def invert_factor(gram_ref, lower_ref, rest_ref, inverse_ref):
    size = gram_ref.shape[0]
    rest_ref[:size, :] = gram_ref[...]
    rest_ref[size:, :] = jnp.zeros((BLOCK, size), jnp.float32)
    row = lax.broadcasted_iota(jnp.int32, (size, size), 0)
    lane = lax.broadcasted_iota(jnp.int32, (size, size), 1)
    inverse_ref[:size, :] = jnp.where(row == lane, 1.0, 0.0)
    inverse_ref[size:, :] = jnp.zeros((BLOCK, size), jnp.float32)

    def body(step, carry):
        rest_cut, inverse_cut = factor_step(rest_ref[:size, :], inverse_ref[:size, :], lower_ref, step * BLOCK)
        rest_ref[:size, :] = pltpu.roll(rest_ref[BLOCK:, :], size - BLOCK, 1) - rest_cut
        inverse_ref[:size, :] = inverse_ref[BLOCK:, :] - inverse_cut
        return carry

    lax.fori_loop(0, size // BLOCK, body, 0)


def inverse_factor(gram):
    size = gram.shape[0]
    return pl.pallas_call(
        invert_factor,
        out_shape=jax.ShapeDtypeStruct((size, size), jnp.float32),
        in_specs=[pl.BlockSpec(memory_space=pltpu.VMEM)],
        out_specs=pl.BlockSpec(memory_space=pltpu.VMEM),
        scratch_shapes=[
            pltpu.VMEM((size + BLOCK, size), jnp.float32),
            pltpu.VMEM((size + BLOCK, size), jnp.float32),
        ],
    )(gram)


def sum_scatter(value, axis):
    count = lax.axis_size(axis)
    if count != 2:
        return lax.psum_scatter(value, axis, scatter_dimension=0, tiled=True)
    here = lax.axis_index(axis)
    rows = value.shape[0] // 2
    sent = lax.dynamic_slice_in_dim(value, (1 - here) * rows, rows, 0)
    got = lax.ppermute(sent, axis, [(0, 1), (1, 0)])
    return lax.dynamic_slice_in_dim(value, here * rows, rows, 0) + got


def gather(value, axis):
    count = lax.axis_size(axis)
    if count != 2:
        return lax.all_gather(value, axis, axis=0, tiled=True)
    other = lax.ppermute(value, axis, [(0, 1), (1, 0)])
    first = lax.axis_index(axis) == 0
    return jnp.concatenate([jnp.where(first, value, other), jnp.where(first, other, value)], 0)


def orth(part):
    gram = lax.dot_general(part, part, (((0,), (0,)), ((), ())), precision=HIGHEST)
    gram = lax.psum(gram, ("row", "col"))
    lower = inverse_factor(gram)
    return lax.dot_general(part, lower, (((1,), (1,)), ((), ())), precision=HIGHEST)


def per_device(counts, row_support, col_support, total, sketch):
    row_local = lax.all_gather(row_support, "col", axis=0, tiled=True)
    col_local = lax.all_gather(col_support, "row", axis=0, tiled=True)
    table = lift(counts, row_local, col_local, total)
    total_rows = table.shape[0] * lax.axis_size("row")
    total_cols = table.shape[1] * lax.axis_size("col")

    first = sum_scatter(jnp.dot(table, sketch, preferred_element_type=jnp.float32), "col")
    q_first = gather(orth(first).astype(jnp.bfloat16), "col")
    partial_value = lax.dot_general(
        table, q_first, (((0,), (0,)), ((), ())), preferred_element_type=jnp.float32
    )
    second = lax.psum_scatter(partial_value, "row", scatter_dimension=0, tiled=True)
    q_second = lax.all_gather(orth(second).astype(jnp.bfloat16), "row", axis=0, tiled=True)
    third = sum_scatter(jnp.dot(table, q_second, preferred_element_type=jnp.float32), "col")
    q_third = gather(orth(third) * jnp.sqrt(jnp.float32(total_rows)), "col")
    return q_third, q_second.astype(jnp.float32) * jnp.sqrt(jnp.float32(total_cols))


def solution(mesh):
    in_specs = (P("row", "col"), P(("row", "col")), P(("col", "row")), P(), P("col", None))
    out_specs = (P("row", None), P("col", None))
    return jax.shard_map(
        per_device, mesh=mesh, in_specs=in_specs, out_specs=out_specs, check_vma=False
    )
```

time: 938 us -> 863 us (0.920)
  other arithmetic: 195 us -> 27.8 us
  waiting for transfers between devices: 528 us -> 644 us
  Pallas kernels: 0 us -> 90.4 us
  matrix products: 121 us -> 51 us
  local copies, waits for them, and re-layouts: 40 us -> 0.06 us
    reduce_scatter x0 -> x1, waiting for transfers between devices: none -> 176 us  [per_device(): lax.psum_scatter(partial_value, 'row', scatter_dimension=0, tiled=True)]
    another operation x27 -> x0, other arithmetic: 163 us -> none  [the longest x20 103 us: factor_of(): return jnp.linalg.cholesky(gram)]
    psum x6 -> x3, waiting for transfers between devices: 528 us -> 377 us  [orth(): gram = lax.psum(gram, ('row', 'col'))]
    pallas_call x0 -> x3, Pallas kernels: none -> 90.4 us  [inverse_factor(): pl.pallas_call(invert_factor, out_shape=jax.ShapeDtypeStruct((size, size)...]
    all_gather x0 -> x1, waiting for transfers between devices: none -> 73.4 us  [per_device(): lax.all_gather(orth(second).astype(jnp.bfloat16), 'row', axis=0, tiled=True)]
    another operation x15 -> x0, matrix products: 40.1 us -> none  [the longest x9 38.7 us: solve_rows(): return jax.scipy.linalg.solve_triangular(lower, matrix.T, lower=True).T]
    dot_general x5 -> x8, matrix products: 65.1 us -> 34.9 us  [the longest x1 11.9 us: per_device(): jnp.dot(table, sketch, preferred_element_type=jnp.float32)]
    unnamed x10 -> x2, local copies, waits for them, and re-layouts: 24.7 us -> 0.01 us
  transfers between devices with their start and end apart: 6 -> 9, of which waited for: 6 -> 8; matrix products, arithmetic and copies ran while one was open for 3% -> 1% of each run, Pallas kernels for 0% -> 0%
where the time goes in v1:
time: 863 us
  waiting for transfers between devices  644 us (75%)
  Pallas kernels  90.4 us (10%)
  matrix products  51 us (6%)
  blocking collectives  28 us (3%)
  other arithmetic  27.8 us (3%)
  between operations  14.6 us (2%)
    psum x3, waiting for transfers between devices, orth(): gram = lax.psum(gram, ('row', 'col'))  377 us
    reduce_scatter x1, waiting for transfers between devices, per_device(): lax.psum_scatter(partial_value, 'row', scatter_dimension=0, tiled=True)  176 us
    pallas_call x3, Pallas kernels, inverse_factor(): pl.pallas_call(invert_factor, out_shape=jax.ShapeDtypeStruct((size, size)...  90.4 us
    all_gather x1, waiting for transfers between devices, per_device(): lax.all_gather(orth(second).astype(jnp.bfloat16), 'row', axis=0, tiled=True)  73.4 us
    all_gather x1, blocking collectives, per_device(): col_local = lax.all_gather(col_support, 'row', axis=0, tiled=True)  22.5 us
  transfers between devices with their start and end apart: 9, of which 8 were waited for; matrix products, arithmetic and copies ran while one was open for 1% of the time, Pallas kernels for 0%

profile of v1, /device:TPU:0, one launch (start us, length us, event | category | flops | bytes accessed | tf_op | source)
XLA Modules:
  0.0 862.6 jit_solution(10863383339941216188)
XLA Ops:
  7.2 0.0 all-reduce.4.cloned.1.call-start
  7.9 5.5 all-gather
  13.4 22.5 %all_gather.10 = s32[16384]{0:T(1024)S(1)} all-gather(s32[1024]{0:T(1024)} %param.7), channel_id=1, replica_groups=mesh['row'=16,'col'=2] {'row'}, dimensions={0}, use_global_device_ids=true | all-gather | bytes 69632 | tf_op jit(solution)/shard_map/all_gather | solution.py:108
  35.9 17.1 %select_convert_fusion = bf16[512,16384]{1,0:T(8,128)(2,1)S(1)} fusion(s32[512,16384]{1,0:T(8,128)} %param.5, f32[16384]{0:T(1024)S(1)} %convert_log_fusion, f32[512]{0:T(512)S(1)} %bitcast.14, f32[]{:T(128)} %bitcast), kind=kLoop, calls=%fused_computation | loop fusion | flops 75497472 | bytes 50399236 | tf_op jit(solution)/shard_map/convert_element_type | solution.py:17
  53.0 0.0 copy-start
  53.0 11.9 %fusion.11 = f32[512,256]{1,0:T(8,128)S(1)} fusion(bf16[512,16384]{1,0:T(8,128)(2,1)S(1)} %select_convert_fusion, bf16[16384,256]{1,0:T(8,128)(2,1)} %param.9), kind=kOutput, calls=%fused_computation.27 | convolution fusion | flops 4294967296 | bytes 25690112 | tf_op jit(solution)/shard_map/dot_general | solution.py:113
  65.0 0.0 copy-done
  65.0 1.6 collective-permute-start
  66.6 7.0 collective-permute-done
  73.6 1.3 fusion.4
  74.9 0.0 all-reduce.4.cloned.1.call-update
  75.0 0.0 reduce-scatter.2.cloned.1.call-start
  75.0 124.0 %all-reduce.4.cloned.1.call-done.gram_ref = f32[256,256]{1,0:T(8,128)} async-done(((f32[256,256]{1,0:T(8,128)}), f32[256,256]{1,0:T(8,128)}) %all-reduce.4.cloned.1.call-update) | async-done | bytes 262160 | tf_op jit(solution)/shard_map/psum | solution.py:101
  199.0 30.1 %shard_map.68 = f32[256,256]{1,0:T(8,128)} custom-call(f32[256,256]{1,0:T(8,128)} %all-reduce.4.cloned.1.call-done.gram_ref), custom_call_target="tpu_custom_call" | custom-call | tf_op jit(solution)/shard_map/pallas_call | solution.py:67
  229.1 1.4 convolution_convert_fusion.1
  230.5 1.5 collective-permute-start.1
  232.0 3.5 collective-permute-done.1
  235.5 16.1 %fusion = f32[16384,256]{1,0:T(8,128)} fusion(bf16[512,16384]{1,0:T(8,128)(2,1)} %copy-done, bf16[256,256]{1,0:T(8,128)(2,1)S(1)} %get-tuple-element.5, bf16[256,256]{1,0:T(8,128)(2,1)S(1)} %get-tuple-element.4), kind=kOutput, calls=%fused_computation.6 | convolution fusion | flops 4295491584 | bytes 33816576 | tf_op jit(solution)/shard_map/dot_general | solution.py:115
  251.6 0.0 reduce-scatter.2.cloned.1.call-update
  251.6 0.2 all-reduce.6.cloned.1.call-start
  251.9 176.3 %reduce-scatter.2.cloned.1.call-done = f32[1024,256]{1,0:T(8,128)} async-done(((f32[16384,256]{1,0:T(8,128)}), f32[1024,256]{1,0:T(8,128)}) %reduce-scatter.2.cloned.1.call-update) | async-done | bytes 1048592 | tf_op jit(solution)/shard_map/reduce_scatter | solution.py:118
  428.2 4.1 fusion.12
  432.2 0.0 all-reduce.6.cloned.1.call-update
  432.3 0.0 all-gather.3.cloned.1.call-start
  432.3 127.6 %all-reduce.6.cloned.1.call-done.gram_ref = f32[256,256]{1,0:T(8,128)} async-done(((f32[256,256]{1,0:T(8,128)}), f32[256,256]{1,0:T(8,128)}) %all-reduce.6.cloned.1.call-update) | async-done | bytes 262160 | tf_op jit(solution)/shard_map/psum | solution.py:101
  560.0 30.2 %shard_map.69 = f32[256,256]{1,0:T(8,128)} custom-call(f32[256,256]{1,0:T(8,128)} %all-reduce.6.cloned.1.call-done.gram_ref), custom_call_target="tpu_custom_call" | custom-call | tf_op jit(solution)/shard_map/pallas_call | solution.py:67
  590.1 3.1 convolution_convert_fusion
  593.2 0.0 all-gather.3.cloned.1.call-update
  593.2 0.0 all-reduce.8.cloned.1.call-start
  593.3 73.4 %all-gather.3.cloned.1.call-done = bf16[16384,256]{1,0:T(8,128)(2,1)} async-done(((bf16[1024,256]{1,0:T(8,128)(2,1)}), bf16[16384,256]{1,0:T(8,128)(2,1)}) %all-gather.3.cloned.1.call-update) | async-done | bytes 8388624 | tf_op jit(solution)/shard_map/all_gather | solution.py:119
  666.7 10.5 %fusion.13 = f32[512,256]{1,0:T(8,128)S(1)} fusion(bf16[512,16384]{1,0:T(8,128)(2,1)} %copy-done, bf16[16384,256]{1,0:T(8,128)(2,1)} %all-gather.3.cloned.1.call-done), kind=kOutput, calls=%fused_computation.29 | convolution fusion | flops 4294967296 | bytes 25690112 | tf_op jit(solution)/shard_map/dot_general | solution.py:120
  677.2 1.5 collective-permute-start.2
  678.8 7.0 collective-permute-done.2
  685.8 1.3 fusion.5
  687.1 0.0 all-reduce.8.cloned.1.call-update
  687.1 125.3 %all-reduce.8.cloned.1.call-done.gram_ref = f32[256,256]{1,0:T(8,128)} async-done(((f32[256,256]{1,0:T(8,128)}), f32[256,256]{1,0:T(8,128)}) %all-reduce.8.cloned.1.call-update) | async-done | bytes 262160 | tf_op jit(solution)/shard_map/psum | solution.py:101
  812.4 30.1 %shard_map.70 = f32[256,256]{1,0:T(8,128)} custom-call(f32[256,256]{1,0:T(8,128)} %all-reduce.8.cloned.1.call-done.gram_ref), custom_call_target="tpu_custom_call" | custom-call | tf_op jit(solution)/shard_map/pallas_call | solution.py:67
  842.6 1.4 convolution_multiply_fusion
  843.9 1.5 collective-permute-start.3
  845.5 9.7 %convert_multiply_fusion = f32[16384,256]{1,0:T(8,128)} fusion(bf16[16384,256]{1,0:T(8,128)(2,1)} %all-gather.3.cloned.1.call-done), kind=kLoop, calls=%fused_computation.1 | loop fusion | flops 8388608 | bytes 25165824 | tf_op jit(solution)/shard_map/mul | solution.py:122
  855.2 0.0 collective-permute-done.3
  855.2 0.8 pad_maximum_fusion
  (6 shorter events, 0.1 us)
Async XLA Ops:
  7.2 191.8 %all-reduce.4.cloned.1.call-start = ((), (), s32[]{:S(2)}) async-start(), calls=%async_computation.1 | async-start | bytes 524288 | tf_op jit(solution)/shard_map/psum | solution.py:101
  53.0 11.9 %copy-start = (bf16[512,16384]{1,0:T(8,128)(2,1)}, bf16[512,16384]{1,0:T(8,128)(2,1)S(1)}, u32[]{:S(2)}) copy-start(bf16[512,16384]{1,0:T(8,128)(2,1)S(1)} %select_convert_fusion) | copy-start | bytes 50331652
  65.0 8.6 collective-permute-start
  75.0 353.2 %reduce-scatter.2.cloned.1.call-start = ((), (), s32[]{:S(2)}) async-start(), calls=%async_computation.2 | async-start | bytes 17825792 | tf_op jit(solution)/shard_map/reduce_scatter | solution.py:118
  230.5 5.0 collective-permute-start.1
  251.6 308.3 %all-reduce.6.cloned.1.call-start = ((), (), s32[]{:S(2)}) async-start(), calls=%async_computation.3 | async-start | bytes 524288 | tf_op jit(solution)/shard_map/psum | solution.py:101
  432.3 234.4 %all-gather.3.cloned.1.call-start = ((), (), s32[]{:S(2)}) async-start(), calls=%async_computation.4 | async-start | bytes 8912896 | tf_op jit(solution)/shard_map/all_gather | solution.py:119
  593.2 219.2 %all-reduce.8.cloned.1.call-start = ((), (), s32[]{:S(2)}) async-start(), calls=%async_computation.5 | async-start | bytes 524288 | tf_op jit(solution)/shard_map/psum | solution.py:101
  677.2 8.5 collective-permute-start.2
  843.9 11.3 %collective-permute-start.3 = (f32[256,256]{1,0:T(8,128)S(1)}, f32[256,256]{1,0:T(8,128)S(1)}, u32[]{:S(2)}, u32[]{:S(2)}) collective-permute-start(f32[256,256]{1,0:T(8,128)S(1)} %convolution_multiply_fusion), channel_id=1, source_target_pairs={{0,1},{1,0},{2,3},{3,2},{4,5},{5,4},{6,7},{7,6},{8,9},{9,8},{10,11... | collective-permute-start | bytes 786440 | tf_op jit(solution)/shard_map/ppermute | solution.py:94
Sparse Core Ops, SparseCore 0:
  75.1 123.8 all-reduce.3
  251.8 176.3 reduce-scatter.1
  434.2 125.6 all-reduce.5
  593.3 73.3 all-gather.2
  687.2 125.1 all-reduce.7

commit v2 on v1

--- a/solution.py
+++ b/solution.py
@@ -1,3 +1,5 @@
+import functools
+
 import jax
 import jax.numpy as jnp
 from jax import lax
@@ -6,6 +8,7 @@
 from jax.sharding import PartitionSpec as P
 
 HIGHEST = lax.Precision.HIGHEST
+MESH = pl.DeviceIdType.MESH
 BLOCK = 32
 
 
@@ -76,6 +79,186 @@
     )(gram)
 
 
+def place(index, cols):
+    return (lax.div(index, cols), lax.rem(index, cols))
+
+
+def greet(count, cols, me):
+    barrier = pltpu.get_barrier_semaphore()
+
+    def hello(step, carry):
+        peer = lax.rem(me + step, count)
+        pl.semaphore_signal(barrier, inc=1, device_id=place(peer, cols), device_id_type=MESH)
+        return carry
+
+    lax.fori_loop(1, count, hello, 0)
+    pl.semaphore_wait(barrier, count - 1)
+
+
+def reduce_kernel(count, cols, part_ref, total_ref, inbox, mine, send_a, recv_a, send_b, recv_b):
+    me = lax.axis_index("row") * cols + lax.axis_index("col")
+    rows = part_ref.shape[0] // count
+    greet(count, cols, me)
+
+    def rows_of(index):
+        return pl.ds(pl.multiple_of(index * rows, rows), rows)
+
+    def scatter_copy(step):
+        peer = lax.rem(me + step, count)
+        return pltpu.make_async_remote_copy(
+            src_ref=part_ref.at[rows_of(peer), :],
+            dst_ref=inbox.at[me],
+            send_sem=send_a.at[step],
+            recv_sem=recv_a.at[me],
+            device_id=place(peer, cols),
+            device_id_type=MESH,
+        )
+
+    def arrival(step):
+        peer = lax.rem(me + count - step, count)
+        return pltpu.make_async_remote_copy(
+            src_ref=part_ref.at[rows_of(me), :],
+            dst_ref=inbox.at[peer],
+            send_sem=send_a.at[step],
+            recv_sem=recv_a.at[peer],
+            device_id=place(peer, cols),
+            device_id_type=MESH,
+        )
+
+    def spread_copy(step):
+        peer = lax.rem(me + step, count)
+        return pltpu.make_async_remote_copy(
+            src_ref=mine,
+            dst_ref=total_ref.at[rows_of(me), :],
+            send_sem=send_b.at[step],
+            recv_sem=recv_b.at[me],
+            device_id=place(peer, cols),
+            device_id_type=MESH,
+        )
+
+    def spread_arrival(step):
+        peer = lax.rem(me + count - step, count)
+        return pltpu.make_async_remote_copy(
+            src_ref=mine,
+            dst_ref=total_ref.at[rows_of(peer), :],
+            send_sem=send_b.at[step],
+            recv_sem=recv_b.at[peer],
+            device_id=place(peer, cols),
+            device_id_type=MESH,
+        )
+
+    def each(action):
+        def body(step, carry):
+            action(step)
+            return carry
+
+        lax.fori_loop(1, count, body, 0)
+
+    each(lambda step: scatter_copy(step).start())
+    inbox[me] = part_ref[rows_of(me), :]
+    each(lambda step: arrival(step).wait_recv())
+    total = inbox[0]
+    for index in range(1, count):
+        total = total + inbox[index]
+    mine[...] = total
+    each(lambda step: spread_copy(step).start())
+    total_ref[rows_of(me), :] = total
+    each(lambda step: spread_arrival(step).wait_recv())
+    each(lambda step: scatter_copy(step).wait_send())
+    each(lambda step: spread_copy(step).wait_send())
+
+
+def whole_sum(value):
+    cols = lax.axis_size("col")
+    count = lax.axis_size("row") * cols
+    size, width = value.shape
+    rows = size // count
+    if size % (8 * count) or width % 128:
+        return lax.psum(value, ("row", "col"))
+    sems = pltpu.SemaphoreType.DMA((count,))
+    return pl.pallas_call(
+        functools.partial(reduce_kernel, count, cols),
+        out_shape=jax.ShapeDtypeStruct(value.shape, value.dtype),
+        in_specs=[pl.BlockSpec(memory_space=pltpu.VMEM)],
+        out_specs=pl.BlockSpec(memory_space=pltpu.VMEM),
+        scratch_shapes=[
+            pltpu.VMEM((count, rows, width), value.dtype),
+            pltpu.VMEM((rows, width), value.dtype),
+            sems,
+            sems,
+            sems,
+            sems,
+        ],
+        compiler_params=pltpu.CompilerParams(collective_id=0, has_side_effects=True),
+    )(value)
+
+
+def support_kernel(n_row, n_col, row_ref, col_ref, row_all, col_all, send_sem, recv_sem):
+    row, col = lax.axis_index("row"), lax.axis_index("col")
+
+    def across(step):
+        return (row, lax.rem(col + step, n_col))
+
+    def down(step):
+        return (lax.rem(row + step, n_row), col)
+
+    barrier = pltpu.get_barrier_semaphore()
+    peers = [across(step) for step in range(1, n_col)] + [down(step) for step in range(1, n_row)]
+    for peer in peers:
+        pl.semaphore_signal(barrier, inc=1, device_id=peer, device_id_type=MESH)
+    pl.semaphore_wait(barrier, len(peers))
+
+    def copy(ref, into, slot, lane, peer):
+        return pltpu.make_async_remote_copy(
+            src_ref=ref,
+            dst_ref=into.at[slot],
+            send_sem=send_sem.at[lane],
+            recv_sem=recv_sem.at[lane],
+            device_id=peer,
+            device_id_type=MESH,
+        )
+
+    sends, waits = [], []
+    for step in range(1, n_col):
+        lane = step - 1
+        sends.append(copy(row_ref, row_all, col, lane, across(step)))
+        waits.append(copy(row_ref, row_all, lax.rem(col + n_col - step, n_col), lane, across(step)))
+    for step in range(1, n_row):
+        lane = n_col - 1 + step - 1
+        sends.append(copy(col_ref, col_all, row, lane, down(step)))
+        waits.append(copy(col_ref, col_all, lax.rem(row + n_row - step, n_row), lane, down(step)))
+    for item in sends:
+        item.start()
+    row_all[col] = row_ref[...]
+    col_all[row] = col_ref[...]
+    for item in waits:
+        item.wait_recv()
+    for item in sends:
+        item.wait_send()
+
+
+def gather_supports(row_support, col_support):
+    n_row, n_col = lax.axis_size("row"), lax.axis_size("col")
+    row_len, col_len = row_support.shape[0], col_support.shape[0]
+    if row_len % 128 or col_len % 128:
+        row_local = lax.all_gather(row_support, "col", axis=0, tiled=True)
+        return row_local, lax.all_gather(col_support, "row", axis=0, tiled=True)
+    lanes = n_row + n_col - 2
+    vmem = pl.BlockSpec(memory_space=pltpu.VMEM)
+    row_all, col_all = pl.pallas_call(
+        functools.partial(support_kernel, n_row, n_col),
+        out_shape=[
+            jax.ShapeDtypeStruct((n_col, row_len // 128, 128), row_support.dtype),
+            jax.ShapeDtypeStruct((n_row, col_len // 128, 128), col_support.dtype),
+        ],
+        in_specs=[vmem, vmem],
+        out_specs=[vmem, vmem],
+        scratch_shapes=[pltpu.SemaphoreType.DMA((lanes,)), pltpu.SemaphoreType.DMA((lanes,))],
+        compiler_params=pltpu.CompilerParams(collective_id=1, has_side_effects=True),
+    )(row_support.reshape(-1, 128), col_support.reshape(-1, 128))
+    return row_all.reshape(-1), col_all.reshape(-1)
+
+
 def sum_scatter(value, axis):
     count = lax.axis_size(axis)
     if count != 2:
@@ -98,14 +281,12 @@
 
 def orth(part):
     gram = lax.dot_general(part, part, (((0,), (0,)), ((), ())), precision=HIGHEST)
-    gram = lax.psum(gram, ("row", "col"))
-    lower = inverse_factor(gram)
+    lower = inverse_factor(whole_sum(gram))
     return lax.dot_general(part, lower, (((1,), (1,)), ((), ())), precision=HIGHEST)
 
 
 def per_device(counts, row_support, col_support, total, sketch):
-    row_local = lax.all_gather(row_support, "col", axis=0, tiled=True)
-    col_local = lax.all_gather(col_support, "row", axis=0, tiled=True)
+    row_local, col_local = gather_supports(row_support, col_support)
     table = lift(counts, row_local, col_local, total)
     total_rows = table.shape[0] * lax.axis_size("row")
     total_cols = table.shape[1] * lax.axis_size("col")

time: 863 us -> 535 us (0.62)
  waiting for transfers between devices: 644 us -> 273 us
  Pallas kernels: 90.4 us -> 161 us
  blocking collectives: 28 us -> 0 us
    psum x3 -> x0, waiting for transfers between devices: 377 us -> none  [orth(): gram = lax.psum(gram, ('row', 'col'))]
    pallas_call x0 -> x4, Pallas kernels: none -> 71.1 us  [the longest x3 60.3 us: whole_sum(): pl.pallas_call(functools.partial(reduce_kernel, count, cols), out_shape=j...]
    all_gather x2 -> x0, blocking collectives: 28 us -> none  [the longest x1 22.5 us: per_device(): col_local = lax.all_gather(col_support, 'row', axis=0, tiled=True)]
  transfers between devices with their start and end apart: 9 -> 6, of which waited for: 8 -> 5; matrix products, arithmetic and copies ran while one was open for 1% -> 2% of each run, Pallas kernels for 0% -> 0%
where the time goes in v2:
time: 535 us; the launch traced here: 534 us
  waiting for transfers between devices  273 us (51%)
  Pallas kernels  161 us (30%)
  matrix products  51 us (10%)
  other arithmetic  29.3 us (5%)
  between operations  14.9 us (3%)
    reduce_scatter x1, waiting for transfers between devices, per_device(): lax.psum_scatter(partial_value, 'row', scatter_dimension=0, tiled=True)  178 us
    pallas_call x3, Pallas kernels, inverse_factor(): pl.pallas_call(invert_factor, out_shape=jax.ShapeDtypeStruct((size, size)...  90.4 us
    all_gather x1, waiting for transfers between devices, per_device(): lax.all_gather(orth(second).astype(jnp.bfloat16), 'row', axis=0, tiled=True)  76 us
    pallas_call x3, Pallas kernels, whole_sum(): pl.pallas_call(functools.partial(reduce_kernel, count, cols), out_shape=j...  60.3 us
    convert_element_type x1, other arithmetic, lift(): jnp.where(block > 0, jnp.maximum(value, 0.0), 0.0).astype(jnp.bfloat16)  17.1 us
    dot_general x1, matrix products, per_device(): lax.dot_general(table, q_first, (((0,), (0,)), ((), ())), preferred_eleme...  16.1 us
    ppermute x2, waiting for transfers between devices, sum_scatter(): got = lax.ppermute(sent, axis, [(0, 1), (1, 0)])  14.4 us
    dot_general x1, matrix products, per_device(): jnp.dot(table, sketch, preferred_element_type=jnp.float32)  11.9 us
  transfers between devices with their start and end apart: 6, of which 5 were waited for; matrix products, arithmetic and copies ran while one was open for 2% of the time, Pallas kernels for 0%

profile of v2, /device:TPU:0, one launch (start us, length us, event | category | flops | bytes accessed | tf_op | source)
XLA Modules:
  0.0 534.3 jit_solution(8639278516167174491)
XLA Ops:
  7.2 0.0 reduce-scatter.2.cloned.1.call-start
  7.9 10.8 %shard_map.68 = (s32[2,2,128]{2,1,0:T(2,128)}, s32[16,8,128]{2,1,0:T(8,128)}) custom-call(s32[2,128]{1,0:T(2,128)} %bitcast.19, s32[8,128]{1,0:T(8,128)} %bitcast.18), custom_call_target="tpu_custom_call" | custom-call | tf_op jit(solution)/shard_map/pallas_call | solution.py:248
  18.7 0.7 convert_log_fusion
  19.4 0.9 log_bitcast_fusion
  20.2 17.1 %select_convert_fusion = bf16[512,16384]{1,0:T(8,128)(2,1)S(1)} fusion(s32[512,16384]{1,0:T(8,128)} %param.5, f32[16384]{0:T(1024)S(1)} %log_bitcast_fusion, f32[512]{0:T(512)S(1)} %bitcast.17, f32[]{:T(128)} %bitcast), kind=kLoop, calls=%fused_computation | loop fusion | flops 75497472 | bytes 50399236 | tf_op jit(solution)/shard_map/convert_element_type | solution.py:20
  37.4 0.0 copy-start
  37.4 11.9 %fusion.11 = f32[512,256]{1,0:T(8,128)S(1)} fusion(bf16[512,16384]{1,0:T(8,128)(2,1)S(1)} %select_convert_fusion, bf16[16384,256]{1,0:T(8,128)(2,1)} %param.9), kind=kOutput, calls=%fused_computation.27 | convolution fusion | flops 4294967296 | bytes 25690112 | tf_op jit(solution)/shard_map/dot_general | solution.py:294
  49.3 0.0 copy-done
  49.3 1.0 collective-permute-start
  50.4 7.4 %collective-permute-done = f32[256,256]{1,0:T(8,128)S(1)} collective-permute-done((f32[256,256]{1,0:T(8,128)S(1)}, f32[256,256]{1,0:T(8,128)S(1)}, u32[]{:S(2)}, u32[]{:S(2)}) %collective-permute-start) | collective-permute-done | bytes 262176 | tf_op jit(solution)/shard_map/ppermute | solution.py:269
  57.7 1.3 fusion.4.part_ref
  59.0 21.1 %shard_map.69.gram_ref = f32[256,256]{1,0:T(8,128)} custom-call(f32[256,256]{1,0:T(8,128)} %fusion.4.part_ref), custom_call_target="tpu_custom_call" | custom-call | tf_op jit(solution)/shard_map/pallas_call | solution.py:179
  80.1 30.1 %shard_map.70 = f32[256,256]{1,0:T(8,128)} custom-call(f32[256,256]{1,0:T(8,128)} %shard_map.69.gram_ref), custom_call_target="tpu_custom_call" | custom-call | tf_op jit(solution)/shard_map/pallas_call | solution.py:70
  110.2 1.4 convolution_convert_fusion.1
  111.6 0.8 collective-permute-start.1
  112.4 4.8 collective-permute-done.1
  117.2 16.1 %fusion = f32[16384,256]{1,0:T(8,128)} fusion(bf16[512,16384]{1,0:T(8,128)(2,1)} %copy-done, bf16[256,256]{1,0:T(8,128)(2,1)S(1)} %get-tuple-element.9, bf16[256,256]{1,0:T(8,128)(2,1)S(1)} %get-tuple-element.8), kind=kOutput, calls=%fused_computation.6 | convolution fusion | flops 4295491584 | bytes 33816576 | tf_op jit(solution)/shard_map/dot_general | solution.py:296
  133.3 0.0 reduce-scatter.2.cloned.1.call-update
  133.4 0.2 all-gather.2.cloned.1.call-start
  133.6 178.0 %reduce-scatter.2.cloned.1.call-done = f32[1024,256]{1,0:T(8,128)} async-done(((f32[16384,256]{1,0:T(8,128)}), f32[1024,256]{1,0:T(8,128)}) %reduce-scatter.2.cloned.1.call-update) | async-done | bytes 1048592 | tf_op jit(solution)/shard_map/reduce_scatter | solution.py:299
  311.6 4.1 fusion.12.part_ref
  315.7 19.8 %shard_map.71.gram_ref = f32[256,256]{1,0:T(8,128)} custom-call(f32[256,256]{1,0:T(8,128)} %fusion.12.part_ref), custom_call_target="tpu_custom_call" | custom-call | tf_op jit(solution)/shard_map/pallas_call | solution.py:179
  335.5 30.1 %shard_map.72 = f32[256,256]{1,0:T(8,128)} custom-call(f32[256,256]{1,0:T(8,128)} %shard_map.71.gram_ref), custom_call_target="tpu_custom_call" | custom-call | tf_op jit(solution)/shard_map/pallas_call | solution.py:70
  365.6 3.1 convolution_convert_fusion
  368.7 0.0 all-gather.2.cloned.1.call-update
  368.7 76.0 %all-gather.2.cloned.1.call-done = bf16[16384,256]{1,0:T(8,128)(2,1)} async-done(((bf16[1024,256]{1,0:T(8,128)(2,1)}), bf16[16384,256]{1,0:T(8,128)(2,1)}) %all-gather.2.cloned.1.call-update) | async-done | bytes 8388624 | tf_op jit(solution)/shard_map/all_gather | solution.py:300
  444.7 10.5 %fusion.13 = f32[512,256]{1,0:T(8,128)S(1)} fusion(bf16[512,16384]{1,0:T(8,128)(2,1)} %copy-done, bf16[16384,256]{1,0:T(8,128)(2,1)} %all-gather.2.cloned.1.call-done), kind=kOutput, calls=%fused_computation.29 | convolution fusion | flops 4294967296 | bytes 25690112 | tf_op jit(solution)/shard_map/dot_general | solution.py:301
  455.3 1.5 collective-permute-start.2
  456.8 7.0 %collective-permute-done.2 = f32[256,256]{1,0:T(8,128)S(1)} collective-permute-done((f32[256,256]{1,0:T(8,128)S(1)}, f32[256,256]{1,0:T(8,128)S(1)}, u32[]{:S(2)}, u32[]{:S(2)}) %collective-permute-start.2) | collective-permute-done | bytes 262176 | tf_op jit(solution)/shard_map/ppermute | solution.py:269
  463.8 1.3 fusion.5.part_ref
  465.1 19.4 %shard_map.73.gram_ref = f32[256,256]{1,0:T(8,128)} custom-call(f32[256,256]{1,0:T(8,128)} %fusion.5.part_ref), custom_call_target="tpu_custom_call" | custom-call | tf_op jit(solution)/shard_map/pallas_call | solution.py:179
  484.6 30.1 %shard_map.74 = f32[256,256]{1,0:T(8,128)} custom-call(f32[256,256]{1,0:T(8,128)} %shard_map.73.gram_ref), custom_call_target="tpu_custom_call" | custom-call | tf_op jit(solution)/shard_map/pallas_call | solution.py:70
  514.7 1.4 convolution_multiply_fusion
  516.1 0.8 collective-permute-start.3
  516.9 9.7 %convert_multiply_fusion = f32[16384,256]{1,0:T(8,128)} fusion(bf16[16384,256]{1,0:T(8,128)(2,1)} %all-gather.2.cloned.1.call-done), kind=kLoop, calls=%fused_computation.1 | loop fusion | flops 8388608 | bytes 25165824 | tf_op jit(solution)/shard_map/mul | solution.py:303
  526.6 0.0 collective-permute-done.3
  526.6 0.8 pad_maximum_fusion
  (4 shorter events, 0.1 us)
Async XLA Ops:
  7.2 304.5 %reduce-scatter.2.cloned.1.call-start = ((), (), s32[]{:S(2)}) async-start(), calls=%async_computation.1 | async-start | bytes 17825792 | tf_op jit(solution)/shard_map/reduce_scatter | solution.py:299
  37.4 11.9 %copy-start = (bf16[512,16384]{1,0:T(8,128)(2,1)}, bf16[512,16384]{1,0:T(8,128)(2,1)S(1)}, u32[]{:S(2)}) copy-start(bf16[512,16384]{1,0:T(8,128)(2,1)S(1)} %select_convert_fusion) | copy-start | bytes 50331652
  49.3 8.4 %collective-permute-start = (f32[256,256]{1,0:T(8,128)S(1)}, f32[256,256]{1,0:T(8,128)S(1)}, u32[]{:S(2)}, u32[]{:S(2)}) collective-permute-start(f32[256,256]{1,0:T(8,128)S(1)} %constant_dynamic-slice_fusion.1), channel_id=1, source_target_pairs={{0,1},{1,0},{2,3},{3,2},{4,5},{5,4},{6,7},{7,6},{8,9},{9,8},{10,11... | collective-permute-start | bytes 786440 | tf_op jit(solution)/shard_map/ppermute | solution.py:269
  111.6 5.6 %collective-permute-start.1 = (bf16[256,256]{1,0:T(8,128)(2,1)S(1)}, bf16[256,256]{1,0:T(8,128)(2,1)S(1)}, u32[]{:S(2)}, u32[]{:S(2)}) collective-permute-start(bf16[256,256]{1,0:T(8,128)(2,1)S(1)} %convolution_convert_fusion.1), channel_id=1, source_target_pairs={{0,1},{1,0},{2,3},{3,2},{4,5},{5,4},{6,7},{7,6},{8,9},{9,8},{10,11... | collective-permute-start | bytes 393224 | tf_op jit(solution)/shard_map/ppermute | solution.py:277
  133.4 311.4 %all-gather.2.cloned.1.call-start = ((), (), s32[]{:S(2)}) async-start(), calls=%async_computation.2 | async-start | bytes 8912896 | tf_op jit(solution)/shard_map/all_gather | solution.py:300
  455.3 8.5 %collective-permute-start.2 = (f32[256,256]{1,0:T(8,128)S(1)}, f32[256,256]{1,0:T(8,128)S(1)}, u32[]{:S(2)}, u32[]{:S(2)}) collective-permute-start(f32[256,256]{1,0:T(8,128)S(1)} %constant_dynamic-slice_fusion), channel_id=1, source_target_pairs={{0,1},{1,0},{2,3},{3,2},{4,5},{5,4},{6,7},{7,6},{8,9},{9,8},{10,11... | collective-permute-start | bytes 786440 | tf_op jit(solution)/shard_map/ppermute | solution.py:269
  516.1 10.5 %collective-permute-start.3 = (f32[256,256]{1,0:T(8,128)S(1)}, f32[256,256]{1,0:T(8,128)S(1)}, u32[]{:S(2)}, u32[]{:S(2)}) collective-permute-start(f32[256,256]{1,0:T(8,128)S(1)} %convolution_multiply_fusion), channel_id=1, source_target_pairs={{0,1},{1,0},{2,3},{3,2},{4,5},{5,4},{6,7},{7,6},{8,9},{9,8},{10,11... | collective-permute-start | bytes 786440 | tf_op jit(solution)/shard_map/ppermute | solution.py:277
Sparse Core Ops, SparseCore 0:
  133.5 178.0 reduce-scatter.1
  368.9 75.8 all-gather.1

commit v3 on v2

--- a/solution.py
+++ b/solution.py
@@ -1,4 +1,5 @@
 import functools
+import math
 
 import jax
 import jax.numpy as jnp
@@ -279,6 +280,42 @@
     return jnp.concatenate([jnp.where(first, value, other), jnp.where(first, other, value)], 0)
 
 
+def digits(count):
+    if count % 4:
+        return [(count, 1)]
+    return [(size, stride) for size, stride in ((count // 4, 4), (2, 2), (2, 1)) if size > 1]
+
+
+def staged_scatter(value, axis, reverse, scale):
+    parts = digits(lax.axis_size(axis))
+    me = lax.axis_index(axis)
+    count = lax.axis_size(axis)
+    rows = value.shape[0] // count
+    value = value.reshape(tuple(size for size, _ in parts) + (rows,) + value.shape[1:])
+    order = list(range(len(parts)))[::-1]
+    if reverse:
+        order = order[:1] + order[1:][::-1]
+    for dim in order:
+        size, stride = parts[dim]
+        own = lax.rem(lax.div(me, stride), size)
+        total = lax.dynamic_index_in_dim(value, own, dim)
+        for step in range(1, size):
+            sent = lax.dynamic_index_in_dim(value, lax.rem(own + step, size), dim)
+            moves = []
+            for source in range(count):
+                digit = source // stride % size
+                moves.append((source, source + ((digit + step) % size - digit) * stride))
+            got = lax.ppermute((sent * scale).astype(jnp.float16), axis, moves)
+            total = total + got.astype(jnp.float32) * (1.0 / scale)
+        value = total
+    return value.reshape((rows,) + value.shape[-1:])
+
+
+def half_scale(rows):
+    bound = 13.0 * math.sqrt(rows) * 1.05
+    return 2.0 ** math.floor(math.log2(65504.0 / bound))
+
+
 def orth(part):
     gram = lax.dot_general(part, part, (((0,), (0,)), ((), ())), precision=HIGHEST)
     lower = inverse_factor(whole_sum(gram))
@@ -296,7 +333,15 @@
     partial_value = lax.dot_general(
         table, q_first, (((0,), (0,)), ((), ())), preferred_element_type=jnp.float32
     )
-    second = lax.psum_scatter(partial_value, "row", scatter_dimension=0, tiled=True)
+    half = partial_value.shape[1] // 2
+    scale = half_scale(total_rows)
+    second = jnp.concatenate(
+        [
+            staged_scatter(partial_value[:, :half], "row", False, scale),
+            staged_scatter(partial_value[:, half:], "row", True, scale),
+        ],
+        1,
+    )
     q_second = lax.all_gather(orth(second).astype(jnp.bfloat16), "row", axis=0, tiled=True)
     third = sum_scatter(jnp.dot(table, q_second, preferred_element_type=jnp.float32), "col")
     q_third = gather(orth(third) * jnp.sqrt(jnp.float32(total_rows)), "col")

time: 535 us -> 451 us (0.84)
  waiting for transfers between devices: 273 us -> 158 us
  other arithmetic: 29.3 us -> 48.4 us
  starting transfers between devices: 4.41 us -> 16.2 us
  matrix products: 51 us -> 41.2 us
  local copies, waits for them, and re-layouts: 0.06 us -> 7.12 us
    reduce_scatter x1 -> x0, waiting for transfers between devices: 178 us -> none  [per_device(): lax.psum_scatter(partial_value, 'row', scatter_dimension=0, tiled=True)]
    ppermute x0 -> x10, waiting for transfers between devices: none -> 61.9 us  [staged_scatter(): got = lax.ppermute((sent * scale).astype(jnp.float16), axis, moves)]
    ppermute x0 -> x10, starting transfers between devices: none -> 12 us  [staged_scatter(): got = lax.ppermute((sent * scale).astype(jnp.float16), axis, moves)]
    add x0 -> x4, other arithmetic: none -> 10.3 us  [staged_scatter(): total = total + got.astype(jnp.float32) * (1.0 / scale)]
    convert_element_type x0 -> x6, other arithmetic: none -> 8.65 us  [staged_scatter(): got = lax.ppermute((sent * scale).astype(jnp.float16), axis, moves)]
    dot_general x1, matrix products: 16.1 us -> 8.19 us  [per_device(): lax.dot_general(table, q_first, (((0,), (0,)), ((), ())), preferred_eleme...]
    slice x0 -> x1, local copies, waits for them, and re-layouts: none -> 6.33 us  [per_device(): partial_value[:, :half]]
  transfers between devices with their start and end apart: 6 -> 15, of which waited for: 5 -> 11; matrix products, arithmetic and copies ran while one was open for 2% -> 6% of each run, Pallas kernels for 0% -> 0%
where the time goes in v3:
time: 451 us; the launch traced here: 450 us
  Pallas kernels  164 us (36%)
  waiting for transfers between devices  158 us (35%)
  other arithmetic  48.4 us (11%)
  matrix products  41.2 us (9%)
  starting transfers between devices  16.2 us (4%)
  between operations  15 us (3%)
  local copies, waits for them, and re-layouts  7.12 us (2%)
    pallas_call x3, Pallas kernels, inverse_factor(): pl.pallas_call(invert_factor, out_shape=jax.ShapeDtypeStruct((size, size)...  90.4 us
    all_gather x1, waiting for transfers between devices, per_device(): lax.all_gather(orth(second).astype(jnp.bfloat16), 'row', axis=0, tiled=True)  76.8 us
    pallas_call x3, Pallas kernels, whole_sum(): pl.pallas_call(functools.partial(reduce_kernel, count, cols), out_shape=j...  62.7 us
    ppermute x10, waiting for transfers between devices, staged_scatter(): got = lax.ppermute((sent * scale).astype(jnp.float16), axis, moves)  61.9 us
    convert_element_type x1, other arithmetic, lift(): jnp.where(block > 0, jnp.maximum(value, 0.0), 0.0).astype(jnp.bfloat16)  17.1 us
    ppermute x2, waiting for transfers between devices, sum_scatter(): got = lax.ppermute(sent, axis, [(0, 1), (1, 0)])  14.4 us
    ppermute x10, starting transfers between devices, staged_scatter(): got = lax.ppermute((sent * scale).astype(jnp.float16), axis, moves)  12 us
    dot_general x1, matrix products, per_device(): jnp.dot(table, sketch, preferred_element_type=jnp.float32)  11.9 us
  transfers between devices with their start and end apart: 15, of which 11 were waited for; matrix products, arithmetic and copies ran while one was open for 6% of the time, Pallas kernels for 0%

profile of v3, /device:TPU:0, one launch (start us, length us, event | category | flops | bytes accessed | tf_op | source)
XLA Modules:
  0.0 449.6 jit_solution(14642099090630657067)
XLA Ops:
  7.2 10.8 %shard_map.68 = (s32[2,2,128]{2,1,0:T(2,128)}, s32[16,8,128]{2,1,0:T(8,128)}) custom-call(s32[2,128]{1,0:T(2,128)} %bitcast.26, s32[8,128]{1,0:T(8,128)} %bitcast.25), custom_call_target="tpu_custom_call" | custom-call | tf_op jit(solution)/shard_map/pallas_call | solution.py:249
  18.0 0.9 log_bitcast_fusion
  18.9 0.7 convert_log_fusion
  20.2 17.1 %select_convert_fusion = bf16[512,16384]{1,0:T(8,128)(2,1)S(1)} fusion(s32[512,16384]{1,0:T(8,128)} %param.5, f32[16384]{0:T(1024)S(1)} %log_bitcast_fusion, f32[512]{0:T(512)S(1)} %bitcast.24, f32[]{:T(128)} %bitcast), kind=kLoop, calls=%fused_computation | loop fusion | flops 75497472 | bytes 50399236 | tf_op jit(solution)/shard_map/convert_element_type | solution.py:21
  37.4 11.9 %fusion.15 = f32[512,256]{1,0:T(8,128)S(1)} fusion(bf16[512,16384]{1,0:T(8,128)(2,1)S(1)} %select_convert_fusion, bf16[16384,256]{1,0:T(8,128)(2,1)} %param.9), kind=kOutput, calls=%fused_computation.48 | convolution fusion | flops 4294967296 | bytes 25690112 | tf_op jit(solution)/shard_map/dot_general | solution.py:331
  49.3 1.0 collective-permute-start
  50.4 7.4 %collective-permute-done = f32[256,256]{1,0:T(8,128)S(1)} collective-permute-done((f32[256,256]{1,0:T(8,128)S(1)}, f32[256,256]{1,0:T(8,128)S(1)}, u32[]{:S(2)}, u32[]{:S(2)}) %collective-permute-start) | collective-permute-done | bytes 262176 | tf_op jit(solution)/shard_map/ppermute | solution.py:270
  57.7 1.3 fusion.5.part_ref
  59.0 21.1 %shard_map.69.gram_ref = f32[256,256]{1,0:T(8,128)} custom-call(f32[256,256]{1,0:T(8,128)} %fusion.5.part_ref), custom_call_target="tpu_custom_call" | custom-call | tf_op jit(solution)/shard_map/pallas_call | solution.py:180
  80.1 30.1 %shard_map.70 = f32[256,256]{1,0:T(8,128)} custom-call(f32[256,256]{1,0:T(8,128)} %shard_map.69.gram_ref), custom_call_target="tpu_custom_call" | custom-call | tf_op jit(solution)/shard_map/pallas_call | solution.py:71
  110.2 1.4 convolution_convert_fusion.1
  111.6 0.8 collective-permute-start.1
  112.4 4.8 %collective-permute-done.1 = bf16[256,256]{1,0:T(8,128)(2,1)S(1)} collective-permute-done((bf16[256,256]{1,0:T(8,128)(2,1)S(1)}, bf16[256,256]{1,0:T(8,128)(2,1)S(1)}, u32[]{:S(2)}, u32[]{:S(2)}) %collective-permute-start.1) | collective-permute-done | bytes 131104 | tf_op jit(solution)/shard_map/ppermute | solution.py:278
  117.3 8.2 %fusion.1 = f32[16384,256]{1,0:T(8,128)S(1)} fusion(bf16[512,16384]{1,0:T(8,128)(2,1)} %copy-done, bf16[256,256]{1,0:T(8,128)(2,1)S(1)} %get-tuple-element.17, bf16[256,256]{1,0:T(8,128)(2,1)S(1)} %get-tuple-element.16), kind=kOutput, calls=%fused_computation.24 | convolution fusion | flops 4295491584 | bytes 33816576 | tf_op jit(solution)/shard_map/dot_general | solution.py:333
  125.5 6.3 %fusion.14 = (f32[16384,128]{1,0:T(8,128)}, f32[16384,128]{1,0:T(8,128)}) fusion(f32[16384,256]{1,0:T(8,128)S(1)} %fusion.1), kind=kLoop, calls=%fused_computation.47 | loop fusion | bytes 33554432 | tf_op jit(solution)/shard_map/slice | solution.py:340
  131.8 4.0 multiply_convert_fusion.1
  135.8 2.6 multiply_convert_fusion
  139.0 1.3 collective-permute-done.2
  140.3 3.3 multiply_add_fusion.1
  143.8 1.3 collective-permute-start.3
  145.1 3.3 multiply_add_fusion
  148.4 1.6 multiply_convert_fusion.5
  150.0 0.7 copy-done.2
  150.7 4.4 collective-permute-start.10
  155.7 12.1 %collective-permute-done.10 = f16[1,2,1,1024,128]{4,3,2,1,0:T(8,128)(2,1)S(1)} collective-permute-done((f16[1,2,1,1024,128]{4,3,2,1,0:T(8,128)(2,1)}, f16[1,2,1,1024,128]{4,3,2,1,0:T(8,128)(2,1)S(1)}, u32[]{:S(2)}, u32[]{:S(2)}) %collective-permute-start.10) | collective-permute-done | bytes 524320 | tf_op jit(solution)/shard_map/ppermute | solution.py:308
  167.8 11.7 %collective-permute-done.8 = f16[1,2,1,1024,128]{4,3,2,1,0:T(8,128)(2,1)S(1)} collective-permute-done((f16[1,2,1,1024,128]{4,3,2,1,0:T(8,128)(2,1)}, f16[1,2,1,1024,128]{4,3,2,1,0:T(8,128)(2,1)S(1)}, u32[]{:S(2)}, u32[]{:S(2)}) %collective-permute-start.8) | collective-permute-done | bytes 524320 | tf_op jit(solution)/shard_map/ppermute | solution.py:308
  179.5 20.4 %collective-permute-done.9 = f16[1,2,1,1024,128]{4,3,2,1,0:T(8,128)(2,1)S(1)} collective-permute-done((f16[1,2,1,1024,128]{4,3,2,1,0:T(8,128)(2,1)S(1)}, f16[1,2,1,1024,128]{4,3,2,1,0:T(8,128)(2,1)S(1)}, u32[]{:S(2)}, u32[]{:S(2)}) %collective-permute-start.9) | collective-permute-done | bytes 524320 | tf_op jit(solution)/shard_map/ppermute | solution.py:308
  199.8 1.5 multiply_add_fusion.3
  201.5 1.2 collective-permute-start.11
  202.7 2.2 multiply_add_fusion.2
  205.1 3.2 collective-permute-start.5
  209.1 7.1 %collective-permute-done.4 = f16[1,1,1,1024,128]{4,3,2,1,0:T(8,128)(2,1)S(1)} collective-permute-done((f16[1,1,1,1024,128]{4,3,2,1,0:T(8,128)(2,1)S(1)}, f16[1,1,1,1024,128]{4,3,2,1,0:T(8,128)(2,1)S(1)}, u32[]{:S(2)}, u32[]{:S(2)}) %collective-permute-start.4) | collective-permute-done | bytes 262176 | tf_op jit(solution)/shard_map/ppermute | solution.py:308
  216.1 9.3 %collective-permute-done.5 = f16[1,1,1,1024,128]{4,3,2,1,0:T(8,128)(2,1)S(1)} collective-permute-done((f16[1,1,1,1024,128]{4,3,2,1,0:T(8,128)(2,1)S(1)}, f16[1,1,1,1024,128]{4,3,2,1,0:T(8,128)(2,1)S(1)}, u32[]{:S(2)}, u32[]{:S(2)}) %collective-permute-start.5) | collective-permute-done | bytes 262176 | tf_op jit(solution)/shard_map/ppermute | solution.py:308
  225.7 2.5 fusion.part_ref
  228.2 22.2 %shard_map.71.gram_ref = f32[256,256]{1,0:T(8,128)} custom-call(f32[256,256]{1,0:T(8,128)} %fusion.part_ref), custom_call_target="tpu_custom_call" | custom-call | tf_op jit(solution)/shard_map/pallas_call | solution.py:180
  250.4 30.1 %shard_map.72 = f32[256,256]{1,0:T(8,128)} custom-call(f32[256,256]{1,0:T(8,128)} %shard_map.71.gram_ref), custom_call_target="tpu_custom_call" | custom-call | tf_op jit(solution)/shard_map/pallas_call | solution.py:71
  280.5 2.8 convolution_convert_fusion
  283.3 76.8 %all-gather.2.cloned.1.call-done = bf16[16384,256]{1,0:T(8,128)(2,1)} async-done(((bf16[1024,256]{1,0:T(8,128)(2,1)}), bf16[16384,256]{1,0:T(8,128)(2,1)}) %all-gather.2.cloned.1.call-update) | async-done | bytes 8388624 | tf_op jit(solution)/shard_map/all_gather | solution.py:345
  360.1 10.5 %fusion.16 = f32[512,256]{1,0:T(8,128)S(1)} fusion(bf16[512,16384]{1,0:T(8,128)(2,1)} %copy-done, bf16[16384,256]{1,0:T(8,128)(2,1)} %all-gather.2.cloned.1.call-done), kind=kOutput, calls=%fused_computation.49 | convolution fusion | flops 4294967296 | bytes 25690112 | tf_op jit(solution)/shard_map/dot_general | solution.py:346
  370.6 1.5 collective-permute-start.12
  372.2 7.0 %collective-permute-done.12 = f32[256,256]{1,0:T(8,128)S(1)} collective-permute-done((f32[256,256]{1,0:T(8,128)S(1)}, f32[256,256]{1,0:T(8,128)S(1)}, u32[]{:S(2)}, u32[]{:S(2)}) %collective-permute-start.12) | collective-permute-done | bytes 262176 | tf_op jit(solution)/shard_map/ppermute | solution.py:270
  379.1 1.3 fusion.6.part_ref
  380.4 19.4 %shard_map.73.gram_ref = f32[256,256]{1,0:T(8,128)} custom-call(f32[256,256]{1,0:T(8,128)} %fusion.6.part_ref), custom_call_target="tpu_custom_call" | custom-call | tf_op jit(solution)/shard_map/pallas_call | solution.py:180
  399.9 30.1 %shard_map.74 = f32[256,256]{1,0:T(8,128)} custom-call(f32[256,256]{1,0:T(8,128)} %shard_map.73.gram_ref), custom_call_target="tpu_custom_call" | custom-call | tf_op jit(solution)/shard_map/pallas_call | solution.py:71
  430.0 1.4 convolution_multiply_fusion
  431.4 0.8 collective-permute-start.13
  432.2 9.7 %convert_multiply_fusion = f32[16384,256]{1,0:T(8,128)} fusion(bf16[16384,256]{1,0:T(8,128)(2,1)} %all-gather.2.cloned.1.call-done), kind=kLoop, calls=%fused_computation.1 | loop fusion | flops 8388608 | bytes 25165824 | tf_op jit(solution)/shard_map/mul | solution.py:348
  442.0 0.8 pad_maximum_fusion.3
  (27 shorter events, 2.8 us)
Async XLA Ops:
  7.2 352.9 %all-gather.2.cloned.1.call-start = ((), (), s32[]{:S(2)}) async-start(), calls=%async_computation | async-start | bytes 8912896 | tf_op jit(solution)/shard_map/all_gather | solution.py:345
  37.4 11.9 %copy-start = (bf16[512,16384]{1,0:T(8,128)(2,1)}, bf16[512,16384]{1,0:T(8,128)(2,1)S(1)}, u32[]{:S(2)}) copy-start(bf16[512,16384]{1,0:T(8,128)(2,1)S(1)} %select_convert_fusion) | copy-start | bytes 50331652
  49.3 8.4 %collective-permute-start = (f32[256,256]{1,0:T(8,128)S(1)}, f32[256,256]{1,0:T(8,128)S(1)}, u32[]{:S(2)}, u32[]{:S(2)}) collective-permute-start(f32[256,256]{1,0:T(8,128)S(1)} %constant_dynamic-slice_fusion.1), channel_id=1, source_target_pairs={{0,1},{1,0},{2,3},{3,2},{4,5},{5,4},{6,7},{7,6},{8,9},{9,8},{10,11... | collective-permute-start | bytes 786440 | tf_op jit(solution)/shard_map/ppermute | solution.py:270
  111.6 5.6 %collective-permute-start.1 = (bf16[256,256]{1,0:T(8,128)(2,1)S(1)}, bf16[256,256]{1,0:T(8,128)(2,1)S(1)}, u32[]{:S(2)}, u32[]{:S(2)}) collective-permute-start(bf16[256,256]{1,0:T(8,128)(2,1)S(1)} %convolution_convert_fusion.1), channel_id=1, source_target_pairs={{0,1},{1,0},{2,3},{3,2},{4,5},{5,4},{6,7},{7,6},{8,9},{9,8},{10,11... | collective-permute-start | bytes 393224 | tf_op jit(solution)/shard_map/ppermute | solution.py:278
  135.8 4.5 %collective-permute-start.2 = (f16[4,2,1,1024,128]{4,3,2,1,0:T(8,128)(2,1)}, f16[4,2,1,1024,128]{4,3,2,1,0:T(8,128)(2,1)}, u32[]{:S(2)}, u32[]{:S(2)}) collective-permute-start(f16[4,2,1,1024,128]{4,3,2,1,0:T(8,128)(2,1)} %multiply_convert_fusion.1), channel_id=1, source_target_pairs={{0,2},{2,0},{4,6},{6,4},{8,10},{10,8},{12,14},{14,12},{16,18},{18,... | collective-permute-start | bytes 6291464 | tf_op jit(solution)/shard_map/ppermute | solution.py:308
  138.4 6.7 %collective-permute-start.7 = (f16[4,2,1,1024,128]{4,3,2,1,0:T(8,128)(2,1)S(1)}, f16[4,2,1,1024,128]{4,3,2,1,0:T(8,128)(2,1)}, u32[]{:S(2)}, u32[]{:S(2)}) collective-permute-start(f16[4,2,1,1024,128]{4,3,2,1,0:T(8,128)(2,1)S(1)} %multiply_convert_fusion), channel_id=1, source_target_pairs={{0,2},{2,0},{4,6},{6,4},{8,10},{10,8},{12,14},{14,12},{16,18},{18,... | collective-permute-start | bytes 6291464 | tf_op jit(solution)/shard_map/ppermute | solution.py:308
  143.6 6.4 %copy-start.1 = (f32[4,2,1,1024,128]{4,3,2,1,0:T(8,128)}, f32[4,2,1,1024,128]{4,3,2,1,0:T(8,128)S(1)}, u32[]{:S(2)}) copy-start(f32[4,2,1,1024,128]{4,3,2,1,0:T(8,128)S(1)} %multiply_add_fusion.1) | copy-start | bytes 12582916
  143.8 58.9 %collective-permute-start.3 = (f16[4,1,1,1024,128]{4,3,2,1,0:T(8,128)(2,1)S(1)}, f16[4,1,1,1024,128]{4,3,2,1,0:T(8,128)(2,1)}, u32[]{:S(2)}, u32[]{:S(2)}) collective-permute-start(f16[4,1,1,1024,128]{4,3,2,1,0:T(8,128)(2,1)S(1)} %multiply_convert_fusion.2), channel_id=1, source_target_pairs={{0,4},{2,6},{4,0},{6,2},{8,12},{10,14},{12,8},{14,10},{16,20},{18,... | collective-permute-start | bytes 3145736 | tf_op jit(solution)/shard_map/ppermute | solution.py:308
  148.4 2.3 copy-start.2
  150.7 17.1 %collective-permute-start.10 = (f16[1,2,1,1024,128]{4,3,2,1,0:T(8,128)(2,1)}, f16[1,2,1,1024,128]{4,3,2,1,0:T(8,128)(2,1)S(1)}, u32[]{:S(2)}, u32[]{:S(2)}) collective-permute-start(f16[1,2,1,1024,128]{4,3,2,1,0:T(8,128)(2,1)} %get-tuple-element.9), channel_id=1, source_target_pairs={{0,24},{2,26},{4,28},{6,30},{8,0},{10,2},{12,4},{14,6},{16,8},{18,... | collective-permute-start | bytes 1572872 | tf_op jit(solution)/shard_map/ppermute | solution.py:308
  155.1 24.4 %collective-permute-start.8 = (f16[1,2,1,1024,128]{4,3,2,1,0:T(8,128)(2,1)}, f16[1,2,1,1024,128]{4,3,2,1,0:T(8,128)(2,1)S(1)}, u32[]{:S(2)}, u32[]{:S(2)}) collective-permute-start(f16[1,2,1,1024,128]{4,3,2,1,0:T(8,128)(2,1)} %get-tuple-element.8), channel_id=1, source_target_pairs={{0,8},{2,10},{4,12},{6,14},{8,16},{10,18},{12,20},{14,22},{16,24},... | collective-permute-start | bytes 1572872 | tf_op jit(solution)/shard_map/ppermute | solution.py:308
  155.1 44.7 %collective-permute-start.9 = (f16[1,2,1,1024,128]{4,3,2,1,0:T(8,128)(2,1)S(1)}, f16[1,2,1,1024,128]{4,3,2,1,0:T(8,128)(2,1)S(1)}, u32[]{:S(2)}, u32[]{:S(2)}) collective-permute-start(f16[1,2,1,1024,128]{4,3,2,1,0:T(8,128)(2,1)S(1)} %get-tuple-element.10), channel_id=1, source_target_pairs={{0,16},{2,18},{4,20},{6,22},{8,24},{10,26},{12,28},{14,30},{16,0},... | collective-permute-start | bytes 1572872 | tf_op jit(solution)/shard_map/ppermute | solution.py:308
  201.5 7.5 %collective-permute-start.11 = (f16[1,1,1,1024,128]{4,3,2,1,0:T(8,128)(2,1)S(1)}, f16[1,1,1,1024,128]{4,3,2,1,0:T(8,128)(2,1)S(1)}, u32[]{:S(2)}, u32[]{:S(2)}) collective-permute-start(f16[1,1,1,1024,128]{4,3,2,1,0:T(8,128)(2,1)S(1)} %multiply_convert_fusion.6), channel_id=1, source_target_pairs={{0,4},{2,6},{4,0},{6,2},{8,12},{10,14},{12,8},{14,10},{16,20},{18,... | collective-permute-start | bytes 786440 | tf_op jit(solution)/shard_map/ppermute | solution.py:308
  205.0 11.1 %collective-permute-start.4 = (f16[1,1,1,1024,128]{4,3,2,1,0:T(8,128)(2,1)S(1)}, f16[1,1,1,1024,128]{4,3,2,1,0:T(8,128)(2,1)S(1)}, u32[]{:S(2)}, u32[]{:S(2)}) collective-permute-start(f16[1,1,1,1024,128]{4,3,2,1,0:T(8,128)(2,1)S(1)} %get-tuple-element.11), channel_id=1, source_target_pairs={{0,8},{2,10},{4,12},{6,14},{8,16},{10,18},{12,20},{14,22},{16,24},... | collective-permute-start | bytes 786440 | tf_op jit(solution)/shard_map/ppermute | solution.py:308
  205.1 20.4 %collective-permute-start.5 = (f16[1,1,1,1024,128]{4,3,2,1,0:T(8,128)(2,1)S(1)}, f16[1,1,1,1024,128]{4,3,2,1,0:T(8,128)(2,1)S(1)}, u32[]{:S(2)}, u32[]{:S(2)}) collective-permute-start(f16[1,1,1,1024,128]{4,3,2,1,0:T(8,128)(2,1)S(1)} %get-tuple-element.13), channel_id=1, source_target_pairs={{0,16},{2,18},{4,20},{6,22},{8,24},{10,26},{12,28},{14,30},{16,0},... | collective-permute-start | bytes 786440 | tf_op jit(solution)/shard_map/ppermute | solution.py:308
  208.3 17.2 %collective-permute-start.6 = (f16[1,1,1,1024,128]{4,3,2,1,0:T(8,128)(2,1)S(1)}, f16[1,1,1,1024,128]{4,3,2,1,0:T(8,128)(2,1)S(1)}, u32[]{:S(2)}, u32[]{:S(2)}) collective-permute-start(f16[1,1,1,1024,128]{4,3,2,1,0:T(8,128)(2,1)S(1)} %get-tuple-element.12), channel_id=1, source_target_pairs={{0,24},{2,26},{4,28},{6,30},{8,0},{10,2},{12,4},{14,6},{16,8},{18,... | collective-permute-start | bytes 786440 | tf_op jit(solution)/shard_map/ppermute | solution.py:308
  370.6 8.5 %collective-permute-start.12 = (f32[256,256]{1,0:T(8,128)S(1)}, f32[256,256]{1,0:T(8,128)S(1)}, u32[]{:S(2)}, u32[]{:S(2)}) collective-permute-start(f32[256,256]{1,0:T(8,128)S(1)} %constant_dynamic-slice_fusion), channel_id=1, source_target_pairs={{0,1},{1,0},{2,3},{3,2},{4,5},{5,4},{6,7},{7,6},{8,9},{9,8},{10,11... | collective-permute-start | bytes 786440 | tf_op jit(solution)/shard_map/ppermute | solution.py:270
  431.4 10.5 %collective-permute-start.13 = (f32[256,256]{1,0:T(8,128)S(1)}, f32[256,256]{1,0:T(8,128)S(1)}, u32[]{:S(2)}, u32[]{:S(2)}) collective-permute-start(f32[256,256]{1,0:T(8,128)S(1)} %convolution_multiply_fusion), channel_id=1, source_target_pairs={{0,1},{1,0},{2,3},{3,2},{4,5},{5,4},{6,7},{7,6},{8,9},{9,8},{10,11... | collective-permute-start | bytes 786440 | tf_op jit(solution)/shard_map/ppermute | solution.py:278
Sparse Core Ops, SparseCore 0:
  283.4 76.5 all-gather.1

commit v4 on v3

--- a/solution.py
+++ b/solution.py
@@ -311,6 +311,31 @@
     return value.reshape((rows,) + value.shape[-1:])
 
 
+def staged_gather(value, axis, reverse):
+    count = lax.axis_size(axis)
+    parts = digits(count)
+    me = lax.axis_index(axis)
+    rows, width = value.shape
+    value = value.reshape((1,) * len(parts) + value.shape)
+    order = list(range(len(parts)))
+    if reverse:
+        order = order[:-1][::-1] + order[-1:]
+    for dim in order:
+        size, stride = parts[dim]
+        own = lax.rem(lax.div(me, stride), size)
+        shape = value.shape[:dim] + (size,) + value.shape[dim + 1 :]
+        whole = lax.dynamic_update_slice_in_dim(jnp.zeros(shape, value.dtype), value, own, dim)
+        for step in range(1, size):
+            moves = []
+            for source in range(count):
+                digit = source // stride % size
+                moves.append((source, source + ((digit + step) % size - digit) * stride))
+            got = lax.ppermute(value, axis, moves)
+            whole = lax.dynamic_update_slice_in_dim(whole, got, lax.rem(own + size - step, size), dim)
+        value = whole
+    return value.reshape(count * rows, width)
+
+
 def half_scale(rows):
     bound = 13.0 * math.sqrt(rows) * 1.05
     return 2.0 ** math.floor(math.log2(65504.0 / bound))
@@ -342,7 +367,10 @@
         ],
         1,
     )
-    q_second = lax.all_gather(orth(second).astype(jnp.bfloat16), "row", axis=0, tiled=True)
+    q_own = orth(second).astype(jnp.bfloat16)
+    q_second = jnp.concatenate(
+        [staged_gather(q_own[:, :half], "row", False), staged_gather(q_own[:, half:], "row", True)], 1
+    )
     third = sum_scatter(jnp.dot(table, q_second, preferred_element_type=jnp.float32), "col")
     q_third = gather(orth(third) * jnp.sqrt(jnp.float32(total_rows)), "col")
     return q_third, q_second.astype(jnp.float32) * jnp.sqrt(jnp.float32(total_cols))

time: 451 us -> 447 us (level)
  waiting for transfers between devices: 158 us -> 127 us
  starting transfers between devices: 16.2 us -> 33.8 us
  local copies, waits for them, and re-layouts: 7.12 us -> 21.2 us
  between operations: 15 us -> 1.74 us
  Pallas kernels: 164 us -> 176 us
    all_gather x1 -> x0, waiting for transfers between devices: 76.8 us -> none  [per_device(): lax.all_gather(orth(second).astype(jnp.bfloat16), 'row', axis=0, tiled=True)]
    ppermute x0 -> x10, waiting for transfers between devices: none -> 46.4 us  [staged_gather(): got = lax.ppermute(value, axis, moves)]
    ppermute x0 -> x10, starting transfers between devices: none -> 17.7 us  [staged_gather(): got = lax.ppermute(value, axis, moves)]
    pallas_call x3, Pallas kernels: 62.7 us -> 75.1 us  [whole_sum(): pl.pallas_call(functools.partial(reduce_kernel, count, cols), out_shape=j...]
    dynamic_update_slice x0 -> x15, local copies, waits for them, and re-layouts: none -> 7.59 us  [the longest x10 3.92 us: staged_gather(): lax.dynamic_update_slice_in_dim(whole, got, lax.rem(own + size - step, si...]
    another operation x0 -> x4, local copies, waits for them, and re-layouts: none -> 6.17 us
  transfers between devices with their start and end apart: 15 -> 24, of which waited for: 11 -> 14; matrix products, arithmetic and copies ran while one was open for 6% -> 8% of each run, Pallas kernels for 0% -> 0%
where the time goes in v4:
time: 447 us; the launch traced here: 446 us
  Pallas kernels  176 us (39%)
  waiting for transfers between devices  127 us (28%)
  other arithmetic  47.7 us (11%)
  matrix products  38 us (9%)
  starting transfers between devices  33.8 us (8%)
  local copies, waits for them, and re-layouts  21.2 us (5%)
    pallas_call x3, Pallas kernels, inverse_factor(): pl.pallas_call(invert_factor, out_shape=jax.ShapeDtypeStruct((size, size)...  90.4 us
    pallas_call x3, Pallas kernels, whole_sum(): pl.pallas_call(functools.partial(reduce_kernel, count, cols), out_shape=j...  75.1 us
    ppermute x10, waiting for transfers between devices, staged_scatter(): got = lax.ppermute((sent * scale).astype(jnp.float16), axis, moves)  61.9 us
    ppermute x10, waiting for transfers between devices, staged_gather(): got = lax.ppermute(value, axis, moves)  46.4 us
    ppermute x10, starting transfers between devices, staged_gather(): got = lax.ppermute(value, axis, moves)  17.7 us
    convert_element_type x1, other arithmetic, lift(): jnp.where(block > 0, jnp.maximum(value, 0.0), 0.0).astype(jnp.bfloat16)  17.1 us
    ppermute x2, waiting for transfers between devices, sum_scatter(): got = lax.ppermute(sent, axis, [(0, 1), (1, 0)])  14.3 us
    ppermute x10, starting transfers between devices, staged_scatter(): got = lax.ppermute((sent * scale).astype(jnp.float16), axis, moves)  12 us
  transfers between devices with their start and end apart: 24, of which 14 were waited for; matrix products, arithmetic and copies ran while one was open for 8% of the time, Pallas kernels for 0%

profile of v4, /device:TPU:0, one launch (start us, length us, event | category | flops | bytes accessed | tf_op | source)
XLA Modules:
  0.0 446.2 jit_solution(4004557441466532289)
XLA Ops:
  0.6 10.8 %shard_map.68 = (s32[2,2,128]{2,1,0:T(2,128)}, s32[16,8,128]{2,1,0:T(8,128)}) custom-call(s32[2,128]{1,0:T(2,128)} %bitcast.37, s32[8,128]{1,0:T(8,128)} %bitcast.36), custom_call_target="tpu_custom_call" | custom-call | tf_op jit(solution)/shard_map/pallas_call | solution.py:249
  13.7 17.1 %select_convert_fusion = bf16[512,16384]{1,0:T(8,128)(2,1)S(1)} fusion(s32[512,16384]{1,0:T(8,128)} %param.5, f32[16384]{0:T(1024)S(1)} %log_bitcast_fusion, f32[512]{0:T(512)S(1)} %bitcast.35, f32[]{:T(128)} %bitcast), kind=kLoop, calls=%fused_computation | loop fusion | flops 75497472 | bytes 50399236 | tf_op jit(solution)/shard_map/convert_element_type | solution.py:21
  30.8 11.9 %fusion.17 = f32[512,256]{1,0:T(8,128)S(1)} fusion(bf16[512,16384]{1,0:T(8,128)(2,1)S(1)} %select_convert_fusion, bf16[16384,256]{1,0:T(8,128)(2,1)} %param.9), kind=kOutput, calls=%fused_computation.69 | convolution fusion | flops 4294967296 | bytes 25690112 | tf_op jit(solution)/shard_map/dot_general | solution.py:356
  43.8 7.4 %collective-permute-done = f32[256,256]{1,0:T(8,128)S(1)} collective-permute-done((f32[256,256]{1,0:T(8,128)S(1)}, f32[256,256]{1,0:T(8,128)S(1)}, u32[]{:S(2)}, u32[]{:S(2)}) %collective-permute-start) | collective-permute-done | bytes 262176 | tf_op jit(solution)/shard_map/ppermute | solution.py:270
  52.5 21.1 %shard_map.69.gram_ref = f32[256,256]{1,0:T(8,128)} custom-call(f32[256,256]{1,0:T(8,128)} %fusion.6.part_ref), custom_call_target="tpu_custom_call" | custom-call | tf_op jit(solution)/shard_map/pallas_call | solution.py:180
  73.5 30.1 %shard_map.70 = f32[256,256]{1,0:T(8,128)} custom-call(f32[256,256]{1,0:T(8,128)} %shard_map.69.gram_ref), custom_call_target="tpu_custom_call" | custom-call | tf_op jit(solution)/shard_map/pallas_call | solution.py:71
  105.8 4.8 %collective-permute-done.1 = bf16[256,256]{1,0:T(8,128)(2,1)S(1)} collective-permute-done((bf16[256,256]{1,0:T(8,128)(2,1)S(1)}, bf16[256,256]{1,0:T(8,128)(2,1)S(1)}, u32[]{:S(2)}, u32[]{:S(2)}) %collective-permute-start.1) | collective-permute-done | bytes 131104 | tf_op jit(solution)/shard_map/ppermute | solution.py:278
  110.7 8.2 %fusion.2 = f32[16384,256]{1,0:T(8,128)S(1)} fusion(bf16[512,16384]{1,0:T(8,128)(2,1)} %copy-done, bf16[256,256]{1,0:T(8,128)(2,1)S(1)} %get-tuple-element.21, bf16[256,256]{1,0:T(8,128)(2,1)S(1)} %get-tuple-element.20), kind=kOutput, calls=%fused_computation.28 | convolution fusion | flops 4295491584 | bytes 33816576 | tf_op jit(solution)/shard_map/dot_general | solution.py:358
  118.9 6.4 %fusion.16 = (f32[16384,128]{1,0:T(8,128)}, f32[16384,128]{1,0:T(8,128)}) fusion(f32[16384,256]{1,0:T(8,128)S(1)} %fusion.2), kind=kLoop, calls=%fused_computation.68 | loop fusion | bytes 33554432 | tf_op jit(solution)/shard_map/slice | solution.py:365
  125.2 4.0 multiply_convert_fusion.1
  129.3 2.6 multiply_convert_fusion
  133.8 3.3 multiply_add_fusion.1
  138.6 3.3 multiply_add_fusion
  141.9 1.5 multiply_convert_fusion.5
  144.2 4.4 collective-permute-start.10
  149.2 12.1 %collective-permute-done.10 = f16[1,2,1,1024,128]{4,3,2,1,0:T(8,128)(2,1)S(1)} collective-permute-done((f16[1,2,1,1024,128]{4,3,2,1,0:T(8,128)(2,1)}, f16[1,2,1,1024,128]{4,3,2,1,0:T(8,128)(2,1)S(1)}, u32[]{:S(2)}, u32[]{:S(2)}) %collective-permute-start.10) | collective-permute-done | bytes 524320 | tf_op jit(solution)/shard_map/ppermute | solution.py:308
  161.3 11.7 %collective-permute-done.8 = f16[1,2,1,1024,128]{4,3,2,1,0:T(8,128)(2,1)S(1)} collective-permute-done((f16[1,2,1,1024,128]{4,3,2,1,0:T(8,128)(2,1)}, f16[1,2,1,1024,128]{4,3,2,1,0:T(8,128)(2,1)S(1)}, u32[]{:S(2)}, u32[]{:S(2)}) %collective-permute-start.8) | collective-permute-done | bytes 524320 | tf_op jit(solution)/shard_map/ppermute | solution.py:308
  173.0 20.4 %collective-permute-done.9 = f16[1,2,1,1024,128]{4,3,2,1,0:T(8,128)(2,1)S(1)} collective-permute-done((f16[1,2,1,1024,128]{4,3,2,1,0:T(8,128)(2,1)S(1)}, f16[1,2,1,1024,128]{4,3,2,1,0:T(8,128)(2,1)S(1)}, u32[]{:S(2)}, u32[]{:S(2)}) %collective-permute-start.9) | collective-permute-done | bytes 524320 | tf_op jit(solution)/shard_map/ppermute | solution.py:308
  193.3 1.5 multiply_add_fusion.3
  196.2 1.5 multiply_add_fusion.2
  198.0 3.2 collective-permute-start.5
  202.6 6.5 %collective-permute-done.4 = f16[1,1,1,1024,128]{4,3,2,1,0:T(8,128)(2,1)S(1)} collective-permute-done((f16[1,1,1,1024,128]{4,3,2,1,0:T(8,128)(2,1)S(1)}, f16[1,1,1,1024,128]{4,3,2,1,0:T(8,128)(2,1)S(1)}, u32[]{:S(2)}, u32[]{:S(2)}) %collective-permute-start.4) | collective-permute-done | bytes 262176 | tf_op jit(solution)/shard_map/ppermute | solution.py:308
  209.0 9.3 %collective-permute-done.5 = f16[1,1,1,1024,128]{4,3,2,1,0:T(8,128)(2,1)S(1)} collective-permute-done((f16[1,1,1,1024,128]{4,3,2,1,0:T(8,128)(2,1)S(1)}, f16[1,1,1,1024,128]{4,3,2,1,0:T(8,128)(2,1)S(1)}, u32[]{:S(2)}, u32[]{:S(2)}) %collective-permute-start.5) | collective-permute-done | bytes 262176 | tf_op jit(solution)/shard_map/ppermute | solution.py:308
  218.6 2.5 fusion.1.part_ref
  221.1 22.1 %shard_map.71.gram_ref = f32[256,256]{1,0:T(8,128)} custom-call(f32[256,256]{1,0:T(8,128)} %fusion.1.part_ref), custom_call_target="tpu_custom_call" | custom-call | tf_op jit(solution)/shard_map/pallas_call | solution.py:180
  243.2 30.1 %shard_map.72 = f32[256,256]{1,0:T(8,128)} custom-call(f32[256,256]{1,0:T(8,128)} %shard_map.71.gram_ref), custom_call_target="tpu_custom_call" | custom-call | tf_op jit(solution)/shard_map/pallas_call | solution.py:71
  273.4 2.0 convolution_convert_fusion
  275.4 3.1 collective-permute-start.12
  278.5 2.8 collective-permute-start.13
  283.0 5.0 %collective-permute-done.12 = bf16[1,1,1,1024,128]{4,3,2,1,0:T(8,128)(2,1)S(1)} collective-permute-done((bf16[1,1,1,1024,128]{4,3,2,1,0:T(8,128)(2,1)S(1)}, bf16[1,1,1,1024,128]{4,3,2,1,0:T(8,128)(2,1)S(1)}, u32[]{:S(2)}, u32[]{:S(2)}) %collective-permute-start.12) | collective-permute-done | bytes 262176 | tf_op jit(solution)/shard_map/ppermute | solution.py:333
  288.1 10.6 %collective-permute-done.13 = bf16[1,1,1,1024,128]{4,3,2,1,0:T(8,128)(2,1)S(1)} collective-permute-done((bf16[1,1,1,1024,128]{4,3,2,1,0:T(8,128)(2,1)S(1)}, bf16[1,1,1,1024,128]{4,3,2,1,0:T(8,128)(2,1)S(1)}, u32[]{:S(2)}, u32[]{:S(2)}) %collective-permute-start.13) | collective-permute-done | bytes 262176 | tf_op jit(solution)/shard_map/ppermute | solution.py:333
  300.1 6.1 %collective-permute-start.18 = (bf16[1,2,1,1024,128]{4,3,2,1,0:T(8,128)(2,1)S(1)}, bf16[1,2,1,1024,128]{4,3,2,1,0:T(8,128)(2,1)S(1)}, u32[]{:S(2)}, u32[]{:S(2)}) collective-permute-start(bf16[1,2,1,1024,128]{4,3,2,1,0:T(8,128)(2,1)S(1)} %constant_dynamic-update-slice_fusion.6), channel_id=1, source_target_pairs={{0,8},{2,10},{4,12},{6,14},{8,16},{10,18},{12,20},{14,22},{16,24},... | collective-permute-start | bytes 1572872 | tf_op jit(solution)/shard_map/ppermute | solution.py:333
  306.7 1.9 collective-permute-start.20
  309.0 10.1 %collective-permute-done.18 = bf16[1,2,1,1024,128]{4,3,2,1,0:T(8,128)(2,1)S(1)} collective-permute-done((bf16[1,2,1,1024,128]{4,3,2,1,0:T(8,128)(2,1)S(1)}, bf16[1,2,1,1024,128]{4,3,2,1,0:T(8,128)(2,1)S(1)}, u32[]{:S(2)}, u32[]{:S(2)}) %collective-permute-start.18) | collective-permute-done | bytes 524320 | tf_op jit(solution)/shard_map/ppermute | solution.py:333
  319.1 20.7 %collective-permute-done.19 = bf16[1,2,1,1024,128]{4,3,2,1,0:T(8,128)(2,1)S(1)} collective-permute-done((bf16[1,2,1,1024,128]{4,3,2,1,0:T(8,128)(2,1)S(1)}, bf16[1,2,1,1024,128]{4,3,2,1,0:T(8,128)(2,1)S(1)}, u32[]{:S(2)}, u32[]{:S(2)}) %collective-permute-start.19) | collective-permute-done | bytes 524320 | tf_op jit(solution)/shard_map/ppermute | solution.py:333
  341.2 2.8 broadcast.37.clone
  344.0 1.7 constant_dynamic-update-slice_fusion.1
  345.7 2.8 broadcast.37.clone.1
  348.5 1.7 constant_dynamic-update-slice_fusion.9
  350.2 1.7 constant_dynamic-update-slice_fusion
  352.0 1.7 constant_dynamic-update-slice_fusion.8
  353.7 8.1 %fusion = f32[512,256]{1,0:T(8,128)S(1)} fusion(bf16[512,16384]{1,0:T(8,128)(2,1)S(1)} %bitcast.30, bf16[16384,128]{1,0:T(8,128)(2,1)} %bitcast.12, bf16[16384,128]{1,0:T(8,128)(2,1)} %bitcast.10), kind=kOutput, calls=%fused_computation.3 | convolution fusion | flops 4311744512 | bytes 25690112 | tf_op jit(solution)/shard_map/dot_general | solution.py:374
  361.8 1.5 collective-permute-start.22
  363.3 7.0 %collective-permute-done.22 = f32[256,256]{1,0:T(8,128)S(1)} collective-permute-done((f32[256,256]{1,0:T(8,128)S(1)}, f32[256,256]{1,0:T(8,128)S(1)}, u32[]{:S(2)}, u32[]{:S(2)}) %collective-permute-start.22) | collective-permute-done | bytes 262176 | tf_op jit(solution)/shard_map/ppermute | solution.py:270
  371.6 31.9 %shard_map.73.gram_ref = f32[256,256]{1,0:T(8,128)} custom-call(f32[256,256]{1,0:T(8,128)} %fusion.7.part_ref), custom_call_target="tpu_custom_call" | custom-call | tf_op jit(solution)/shard_map/pallas_call | solution.py:180
  403.5 30.1 %shard_map.74 = f32[256,256]{1,0:T(8,128)} custom-call(f32[256,256]{1,0:T(8,128)} %shard_map.73.gram_ref), custom_call_target="tpu_custom_call" | custom-call | tf_op jit(solution)/shard_map/pallas_call | solution.py:71
  433.6 1.4 convolution_multiply_fusion
  435.8 9.6 %convert_multiply_fusion = f32[16384,256]{1,0:T(8,128)} fusion(bf16[16384,128]{1,0:T(8,128)(2,1)} %bitcast.12, bf16[16384,128]{1,0:T(8,128)(2,1)} %bitcast.10), kind=kLoop, calls=%fused_computation.1 | loop fusion | flops 20971520 | bytes 25165824 | tf_op jit(solution)/shard_map/mul | solution.py:376
  (77 shorter events, 22.4 us)
Async XLA Ops:
  30.8 11.9 %copy-start = (bf16[512,16384]{1,0:T(8,128)(2,1)}, bf16[512,16384]{1,0:T(8,128)(2,1)S(1)}, u32[]{:S(2)}) copy-start(bf16[512,16384]{1,0:T(8,128)(2,1)S(1)} %select_convert_fusion) | copy-start | bytes 50331652
  42.8 8.4 %collective-permute-start = (f32[256,256]{1,0:T(8,128)S(1)}, f32[256,256]{1,0:T(8,128)S(1)}, u32[]{:S(2)}, u32[]{:S(2)}) collective-permute-start(f32[256,256]{1,0:T(8,128)S(1)} %constant_dynamic-slice_fusion.1), channel_id=1, source_target_pairs={{0,1},{1,0},{2,3},{3,2},{4,5},{5,4},{6,7},{7,6},{8,9},{9,8},{10,11... | collective-permute-start | bytes 786440 | tf_op jit(solution)/shard_map/ppermute | solution.py:270
  105.0 5.6 %collective-permute-start.1 = (bf16[256,256]{1,0:T(8,128)(2,1)S(1)}, bf16[256,256]{1,0:T(8,128)(2,1)S(1)}, u32[]{:S(2)}, u32[]{:S(2)}) collective-permute-start(bf16[256,256]{1,0:T(8,128)(2,1)S(1)} %convolution_convert_fusion.1), channel_id=1, source_target_pairs={{0,1},{1,0},{2,3},{3,2},{4,5},{5,4},{6,7},{7,6},{8,9},{9,8},{10,11... | collective-permute-start | bytes 393224 | tf_op jit(solution)/shard_map/ppermute | solution.py:278
  129.3 4.5 %collective-permute-start.2 = (f16[4,2,1,1024,128]{4,3,2,1,0:T(8,128)(2,1)}, f16[4,2,1,1024,128]{4,3,2,1,0:T(8,128)(2,1)}, u32[]{:S(2)}, u32[]{:S(2)}) collective-permute-start(f16[4,2,1,1024,128]{4,3,2,1,0:T(8,128)(2,1)} %multiply_convert_fusion.1), channel_id=1, source_target_pairs={{0,2},{2,0},{4,6},{6,4},{8,10},{10,8},{12,14},{14,12},{16,18},{18,... | collective-permute-start | bytes 6291464 | tf_op jit(solution)/shard_map/ppermute | solution.py:308
  131.9 6.7 %collective-permute-start.7 = (f16[4,2,1,1024,128]{4,3,2,1,0:T(8,128)(2,1)S(1)}, f16[4,2,1,1024,128]{4,3,2,1,0:T(8,128)(2,1)}, u32[]{:S(2)}, u32[]{:S(2)}) collective-permute-start(f16[4,2,1,1024,128]{4,3,2,1,0:T(8,128)(2,1)S(1)} %multiply_convert_fusion), channel_id=1, source_target_pairs={{0,2},{2,0},{4,6},{6,4},{8,10},{10,8},{12,14},{14,12},{16,18},{18,... | collective-permute-start | bytes 6291464 | tf_op jit(solution)/shard_map/ppermute | solution.py:308
  137.1 4.8 %copy-start.1 = (f32[4,2,1,1024,128]{4,3,2,1,0:T(8,128)}, f32[4,2,1,1024,128]{4,3,2,1,0:T(8,128)S(1)}, u32[]{:S(2)}) copy-start(f32[4,2,1,1024,128]{4,3,2,1,0:T(8,128)S(1)} %multiply_add_fusion.1) | copy-start | bytes 12582916
  137.3 58.9 %collective-permute-start.3 = (f16[4,1,1,1024,128]{4,3,2,1,0:T(8,128)(2,1)S(1)}, f16[4,1,1,1024,128]{4,3,2,1,0:T(8,128)(2,1)}, u32[]{:S(2)}, u32[]{:S(2)}) collective-permute-start(f16[4,1,1,1024,128]{4,3,2,1,0:T(8,128)(2,1)S(1)} %multiply_convert_fusion.2), channel_id=1, source_target_pairs={{0,4},{2,6},{4,0},{6,2},{8,12},{10,14},{12,8},{14,10},{16,20},{18,... | collective-permute-start | bytes 3145736 | tf_op jit(solution)/shard_map/ppermute | solution.py:308
  141.9 2.3 copy-start.3
  144.2 17.1 %collective-permute-start.10 = (f16[1,2,1,1024,128]{4,3,2,1,0:T(8,128)(2,1)}, f16[1,2,1,1024,128]{4,3,2,1,0:T(8,128)(2,1)S(1)}, u32[]{:S(2)}, u32[]{:S(2)}) collective-permute-start(f16[1,2,1,1024,128]{4,3,2,1,0:T(8,128)(2,1)} %get-tuple-element.9), channel_id=1, source_target_pairs={{0,24},{2,26},{4,28},{6,30},{8,0},{10,2},{12,4},{14,6},{16,8},{18,... | collective-permute-start | bytes 1572872 | tf_op jit(solution)/shard_map/ppermute | solution.py:308
  148.6 24.4 %collective-permute-start.8 = (f16[1,2,1,1024,128]{4,3,2,1,0:T(8,128)(2,1)}, f16[1,2,1,1024,128]{4,3,2,1,0:T(8,128)(2,1)S(1)}, u32[]{:S(2)}, u32[]{:S(2)}) collective-permute-start(f16[1,2,1,1024,128]{4,3,2,1,0:T(8,128)(2,1)} %get-tuple-element.8), channel_id=1, source_target_pairs={{0,8},{2,10},{4,12},{6,14},{8,16},{10,18},{12,20},{14,22},{16,24},... | collective-permute-start | bytes 1572872 | tf_op jit(solution)/shard_map/ppermute | solution.py:308
  148.6 44.7 %collective-permute-start.9 = (f16[1,2,1,1024,128]{4,3,2,1,0:T(8,128)(2,1)S(1)}, f16[1,2,1,1024,128]{4,3,2,1,0:T(8,128)(2,1)S(1)}, u32[]{:S(2)}, u32[]{:S(2)}) collective-permute-start(f16[1,2,1,1024,128]{4,3,2,1,0:T(8,128)(2,1)S(1)} %get-tuple-element.10), channel_id=1, source_target_pairs={{0,16},{2,18},{4,20},{6,22},{8,24},{10,26},{12,28},{14,30},{16,0},... | collective-permute-start | bytes 1572872 | tf_op jit(solution)/shard_map/ppermute | solution.py:308
  149.2 47.0 %copy-start.2 = (f32[4,2,1,1024,128]{4,3,2,1,0:T(8,128)S(1)}, f32[4,2,1,1024,128]{4,3,2,1,0:T(8,128)}, u32[]{:S(2)}) copy-start(f32[4,2,1,1024,128]{4,3,2,1,0:T(8,128)} %copy-done.1) | copy-start | bytes 12582916
  195.0 7.5 %collective-permute-start.11 = (f16[1,1,1,1024,128]{4,3,2,1,0:T(8,128)(2,1)S(1)}, f16[1,1,1,1024,128]{4,3,2,1,0:T(8,128)(2,1)S(1)}, u32[]{:S(2)}, u32[]{:S(2)}) collective-permute-start(f16[1,1,1,1024,128]{4,3,2,1,0:T(8,128)(2,1)S(1)} %multiply_convert_fusion.6), channel_id=1, source_target_pairs={{0,4},{2,6},{4,0},{6,2},{8,12},{10,14},{12,8},{14,10},{16,20},{18,... | collective-permute-start | bytes 786440 | tf_op jit(solution)/shard_map/ppermute | solution.py:308
  197.9 11.1 %collective-permute-start.4 = (f16[1,1,1,1024,128]{4,3,2,1,0:T(8,128)(2,1)S(1)}, f16[1,1,1,1024,128]{4,3,2,1,0:T(8,128)(2,1)S(1)}, u32[]{:S(2)}, u32[]{:S(2)}) collective-permute-start(f16[1,1,1,1024,128]{4,3,2,1,0:T(8,128)(2,1)S(1)} %get-tuple-element.11), channel_id=1, source_target_pairs={{0,8},{2,10},{4,12},{6,14},{8,16},{10,18},{12,20},{14,22},{16,24},... | collective-permute-start | bytes 786440 | tf_op jit(solution)/shard_map/ppermute | solution.py:308
  198.0 20.4 %collective-permute-start.5 = (f16[1,1,1,1024,128]{4,3,2,1,0:T(8,128)(2,1)S(1)}, f16[1,1,1,1024,128]{4,3,2,1,0:T(8,128)(2,1)S(1)}, u32[]{:S(2)}, u32[]{:S(2)}) collective-permute-start(f16[1,1,1,1024,128]{4,3,2,1,0:T(8,128)(2,1)S(1)} %get-tuple-element.13), channel_id=1, source_target_pairs={{0,16},{2,18},{4,20},{6,22},{8,24},{10,26},{12,28},{14,30},{16,0},... | collective-permute-start | bytes 786440 | tf_op jit(solution)/shard_map/ppermute | solution.py:308
  201.2 17.2 %collective-permute-start.6 = (f16[1,1,1,1024,128]{4,3,2,1,0:T(8,128)(2,1)S(1)}, f16[1,1,1,1024,128]{4,3,2,1,0:T(8,128)(2,1)S(1)}, u32[]{:S(2)}, u32[]{:S(2)}) collective-permute-start(f16[1,1,1,1024,128]{4,3,2,1,0:T(8,128)(2,1)S(1)} %get-tuple-element.12), channel_id=1, source_target_pairs={{0,24},{2,26},{4,28},{6,30},{8,0},{10,2},{12,4},{14,6},{16,8},{18,... | collective-permute-start | bytes 786440 | tf_op jit(solution)/shard_map/ppermute | solution.py:308
  275.4 12.6 %collective-permute-start.12 = (bf16[1,1,1,1024,128]{4,3,2,1,0:T(8,128)(2,1)S(1)}, bf16[1,1,1,1024,128]{4,3,2,1,0:T(8,128)(2,1)S(1)}, u32[]{:S(2)}, u32[]{:S(2)}) collective-permute-start(bf16[1,1,1,1024,128]{4,3,2,1,0:T(8,128)(2,1)S(1)} %get-tuple-element.16), channel_id=1, source_target_pairs={{0,8},{2,10},{4,12},{6,14},{8,16},{10,18},{12,20},{14,22},{16,24},... | collective-permute-start | bytes 786440 | tf_op jit(solution)/shard_map/ppermute | solution.py:333
  278.5 20.2 %collective-permute-start.13 = (bf16[1,1,1,1024,128]{4,3,2,1,0:T(8,128)(2,1)S(1)}, bf16[1,1,1,1024,128]{4,3,2,1,0:T(8,128)(2,1)S(1)}, u32[]{:S(2)}, u32[]{:S(2)}) collective-permute-start(bf16[1,1,1,1024,128]{4,3,2,1,0:T(8,128)(2,1)S(1)} %get-tuple-element.16), channel_id=1, source_target_pairs={{0,16},{2,18},{4,20},{6,22},{8,24},{10,26},{12,28},{14,30},{16,0},... | collective-permute-start | bytes 786440 | tf_op jit(solution)/shard_map/ppermute | solution.py:333
  281.3 17.4 %collective-permute-start.14 = (bf16[1,1,1,1024,128]{4,3,2,1,0:T(8,128)(2,1)S(1)}, bf16[1,1,1,1024,128]{4,3,2,1,0:T(8,128)(2,1)S(1)}, u32[]{:S(2)}, u32[]{:S(2)}) collective-permute-start(bf16[1,1,1,1024,128]{4,3,2,1,0:T(8,128)(2,1)S(1)} %get-tuple-element.16), channel_id=1, source_target_pairs={{0,24},{2,26},{4,28},{6,30},{8,0},{10,2},{12,4},{14,6},{16,8},{18,... | collective-permute-start | bytes 786440 | tf_op jit(solution)/shard_map/ppermute | solution.py:333
  281.5 18.5 %collective-permute-start.17 = (bf16[1,1,1,1024,128]{4,3,2,1,0:T(8,128)(2,1)S(1)}, bf16[1,1,1,1024,128]{4,3,2,1,0:T(8,128)(2,1)S(1)}, u32[]{:S(2)}, u32[]{:S(2)}) collective-permute-start(bf16[1,1,1,1024,128]{4,3,2,1,0:T(8,128)(2,1)S(1)} %get-tuple-element.17), channel_id=1, source_target_pairs={{0,4},{2,6},{4,0},{6,2},{8,12},{10,14},{12,8},{14,10},{16,20},{18,... | collective-permute-start | bytes 786440 | tf_op jit(solution)/shard_map/ppermute | solution.py:333
  298.8 41.7 %collective-permute-start.15 = (bf16[4,1,1,1024,128]{4,3,2,1,0:T(8,128)(2,1)S(1)}, bf16[4,1,1,1024,128]{4,3,2,1,0:T(8,128)(2,1)S(1)}, u32[]{:S(2)}, u32[]{:S(2)}) collective-permute-start(bf16[4,1,1,1024,128]{4,3,2,1,0:T(8,128)(2,1)S(1)} %constant_dynamic-update-slice_fusion.12), channel_id=1, source_target_pairs={{0,4},{2,6},{4,0},{6,2},{8,12},{10,14},{12,8},{14,10},{16,20},{18,... | collective-permute-start | bytes 3145736 | tf_op jit(solution)/shard_map/ppermute | solution.py:333
  300.1 18.9 %collective-permute-start.18 = (bf16[1,2,1,1024,128]{4,3,2,1,0:T(8,128)(2,1)S(1)}, bf16[1,2,1,1024,128]{4,3,2,1,0:T(8,128)(2,1)S(1)}, u32[]{:S(2)}, u32[]{:S(2)}) collective-permute-start(bf16[1,2,1,1024,128]{4,3,2,1,0:T(8,128)(2,1)S(1)} %constant_dynamic-update-slice_fusion.6), channel_id=1, source_target_pairs={{0,8},{2,10},{4,12},{6,14},{8,16},{10,18},{12,20},{14,22},{16,24},... | collective-permute-start | bytes 1572872 | tf_op jit(solution)/shard_map/ppermute | solution.py:333
  306.2 33.6 %collective-permute-start.19 = (bf16[1,2,1,1024,128]{4,3,2,1,0:T(8,128)(2,1)S(1)}, bf16[1,2,1,1024,128]{4,3,2,1,0:T(8,128)(2,1)S(1)}, u32[]{:S(2)}, u32[]{:S(2)}) collective-permute-start(bf16[1,2,1,1024,128]{4,3,2,1,0:T(8,128)(2,1)S(1)} %constant_dynamic-update-slice_fusion.6), channel_id=1, source_target_pairs={{0,16},{2,18},{4,20},{6,22},{8,24},{10,26},{12,28},{14,30},{16,0},... | collective-permute-start | bytes 1572872 | tf_op jit(solution)/shard_map/ppermute | solution.py:333
  306.7 33.2 %collective-permute-start.20 = (bf16[1,2,1,1024,128]{4,3,2,1,0:T(8,128)(2,1)S(1)}, bf16[1,2,1,1024,128]{4,3,2,1,0:T(8,128)(2,1)S(1)}, u32[]{:S(2)}, u32[]{:S(2)}) collective-permute-start(bf16[1,2,1,1024,128]{4,3,2,1,0:T(8,128)(2,1)S(1)} %constant_dynamic-update-slice_fusion.6), channel_id=1, source_target_pairs={{0,24},{2,26},{4,28},{6,30},{8,0},{10,2},{12,4},{14,6},{16,8},{18,... | collective-permute-start | bytes 1572872 | tf_op jit(solution)/shard_map/ppermute | solution.py:333
  340.0 10.3 %collective-permute-start.21 = (bf16[4,2,1,1024,128]{4,3,2,1,0:T(8,128)(2,1)S(1)}, bf16[4,2,1,1024,128]{4,3,2,1,0:T(8,128)(2,1)S(1)}, u32[]{:S(2)}, u32[]{:S(2)}) collective-permute-start(bf16[4,2,1,1024,128]{4,3,2,1,0:T(8,128)(2,1)S(1)} %constant_dynamic-update-slice_fusion.2), channel_id=1, source_target_pairs={{0,2},{2,0},{4,6},{6,4},{8,10},{10,8},{12,14},{14,12},{16,18},{18,... | collective-permute-start | bytes 6291464 | tf_op jit(solution)/shard_map/ppermute | solution.py:333
  340.0 13.6 %slice-start = ((s8[16777216]{0:T(1024)(128)(4,1)}), s8[4194304]{0:T(1024)(128)(4,1)S(1)}, s32[]{:S(2)}) async-start(s8[16777216]{0:T(1024)(128)(4,1)} %bitcast.29), calls=%async_computation | async-start | bytes 8388608
  340.6 13.0 %slice-start.1 = ((s8[16777216]{0:T(1024)(128)(4,1)}), s8[4194304]{0:T(1024)(128)(4,1)S(1)}, s32[]{:S(2)}) async-start(s8[16777216]{0:T(1024)(128)(4,1)} %bitcast.29), calls=%async_computation.1 | async-start | bytes 8388608
  340.7 11.3 %collective-permute-start.16 = (bf16[4,2,1,1024,128]{4,3,2,1,0:T(8,128)(2,1)S(1)}, bf16[4,2,1,1024,128]{4,3,2,1,0:T(8,128)(2,1)S(1)}, u32[]{:S(2)}, u32[]{:S(2)}) collective-permute-start(bf16[4,2,1,1024,128]{4,3,2,1,0:T(8,128)(2,1)S(1)} %constant_dynamic-update-slice_fusion.10), channel_id=1, source_target_pairs={{0,2},{2,0},{4,6},{6,4},{8,10},{10,8},{12,14},{14,12},{16,18},{18,... | collective-permute-start | bytes 6291464 | tf_op jit(solution)/shard_map/ppermute | solution.py:333
  345.7 8.0 %slice-start.2 = ((s8[16777216]{0:T(1024)(128)(4,1)}), s8[4194304]{0:T(1024)(128)(4,1)S(1)}, s32[]{:S(2)}) async-start(s8[16777216]{0:T(1024)(128)(4,1)} %bitcast.29), calls=%async_computation.2 | async-start | bytes 8388608
  350.2 3.4 slice-start.3
  361.8 8.5 %collective-permute-start.22 = (f32[256,256]{1,0:T(8,128)S(1)}, f32[256,256]{1,0:T(8,128)S(1)}, u32[]{:S(2)}, u32[]{:S(2)}) collective-permute-start(f32[256,256]{1,0:T(8,128)S(1)} %constant_dynamic-slice_fusion), channel_id=1, source_target_pairs={{0,1},{1,0},{2,3},{3,2},{4,5},{5,4},{6,7},{7,6},{8,9},{9,8},{10,11... | collective-permute-start | bytes 786440 | tf_op jit(solution)/shard_map/ppermute | solution.py:270
  435.0 10.4 %collective-permute-start.23 = (f32[256,256]{1,0:T(8,128)S(1)}, f32[256,256]{1,0:T(8,128)S(1)}, u32[]{:S(2)}, u32[]{:S(2)}) collective-permute-start(f32[256,256]{1,0:T(8,128)S(1)} %convolution_multiply_fusion), channel_id=1, source_target_pairs={{0,1},{1,0},{2,3},{3,2},{4,5},{5,4},{6,7},{7,6},{8,9},{9,8},{10,11... | collective-permute-start | bytes 786440 | tf_op jit(solution)/shard_map/ppermute | solution.py:278
